TPU v7x, 512 devices: a whole 4x8x8 slice. The times are simulated.
512 devices in a mesh: dp: 32 (over x, y), expert: 2 (over core), ffn: 8 (over z).
Axes of the slice: x: 4, y: 8, z: 8, core: 2. Of those that a mesh axis runs over, the one named last changes fastest.
Arguments:
- grad_rows: bfloat16 [4096, 6144], P('dp', 'ffn'), may hold values from -80 to 80
- gate_probs: float32 [4096, 2], P('dp'), may hold values from 0.1 to 1
- expert_ids: int32 [4096, 2], P('dp'), may hold values from 0 to 3, all different within a row; in each aligned block of 128 rows (0 to 127, 128 to 255, ...) at most 72 rows name the same one
- gate_pre: bfloat16 [4, 2304, 8192], P('expert', 'ffn', 'dp'), may hold values from -6 to 6
- up_pre: bfloat16 [4, 2304, 8192], P('expert', 'ffn', 'dp'), may hold values from -40 to 40
- down_weight: bfloat16 [4, 8192, 6144], P('expert', 'dp', 'ffn'), may hold values from -0.0625 to 0.0625
Outputs:
- down_grad: bfloat16 [4, 8192, 6144], P('expert', 'dp', 'ffn')
- gate_grad: bfloat16 [4, 2304, 8192], P('expert', 'ffn', 'dp')
- up_grad: bfloat16 [4, 2304, 8192], P('expert', 'ffn', 'dp')
Inputs may be any that keep to these rules, and one draw needn't show every extreme that they name: `expert_ids`: in the 128 tokens of one index of dp no expert is named by more than 72 routes, a bound that some block reaches; a token's two routes name different experts.
All inputs are finite; a program needn't handle non-finite values.
Results may differ from a plain program's by a relative error of at most 0.019.
Values may be sent and summed in bfloat16 or wider, within the bound.
No kernel may reach another device: no remote copies, remote signals or barrier semaphores. Data moves between devices by JAX's collectives and lax.ppermute only.
A program may use at most 64 MiB of HBM per device.

v0:
```python
import math

import jax
import jax.numpy as jnp
from jax import lax
from jax.sharding import PartitionSpec as P

CAP = 72


def slot_table(route_ids, experts_total):
    tokens_here, routes = route_ids.shape
    flat_ids = route_ids.reshape(tokens_here * routes)
    one_hot = (flat_ids[:, None] == jnp.arange(experts_total, dtype=jnp.int32)[None, :]).astype(
        jnp.int32
    )
    earlier = jnp.cumsum(one_hot, axis=0) - one_hot
    return jnp.sum(earlier * one_hot, axis=1).reshape(tokens_here, routes)


def on_device(grad_rows, gate_probs, expert_ids, gate_pre, up_pre, down_weight):
    experts_here, rows_here, hidden_width = gate_pre.shape
    feature_width = down_weight.shape[2]
    capacity = CAP
    experts_total = experts_here * lax.axis_size("expert")
    slot_index = slot_table(expert_ids, experts_total)
    first_expert = lax.axis_index("expert") * experts_here
    local_ids = expert_ids - first_expert
    expert_match = (
        local_ids[:, :, None] == jnp.arange(experts_here, dtype=jnp.int32)[None, None, :]
    ).astype(jnp.float32)
    expert_match = expert_match * gate_probs[:, :, None]
    slot_match = (
        slot_index[:, :, None] == jnp.arange(capacity, dtype=jnp.int32)[None, None, :]
    ).astype(jnp.float32)
    placing = jnp.einsum("tke,tks->est", expert_match, slot_match, precision=lax.Precision.HIGHEST)
    dispatched = jnp.einsum(
        "est,td->esd", placing, grad_rows.astype(jnp.float32), precision=lax.Precision.HIGHEST
    ).astype(jnp.bfloat16)
    arrived = lax.all_gather(dispatched, "dp", axis=1, tiled=True)
    gate_value = gate_pre.astype(jnp.float32)
    up_value = up_pre.astype(jnp.float32)
    sigmoid_gate = jax.nn.sigmoid(gate_value)
    silu_gate = gate_value * sigmoid_gate
    hidden = (silu_gate * up_value).astype(jnp.bfloat16)
    partial_sums = jnp.einsum(
        "erd,efd->erf", arrived, down_weight, preferred_element_type=jnp.float32
    )
    own_rows = lax.psum_scatter(
        partial_sums.astype(jnp.bfloat16), "ffn", scatter_dimension=1, tiled=True
    ).astype(jnp.float32)
    gate_grad = (
        own_rows * up_value * sigmoid_gate * (1.0 + gate_value * (1.0 - sigmoid_gate))
    ).astype(jnp.bfloat16)
    up_grad = (own_rows * silu_gate).astype(jnp.bfloat16)
    weight_grad = jnp.einsum(
        "erf,erd->efd",
        lax.all_gather(hidden, "ffn", axis=1, tiled=True),
        arrived,
        preferred_element_type=jnp.float32,
    )
    squares = lax.psum(jnp.sum(weight_grad * weight_grad), ("dp", "expert", "ffn"))
    entry_count = (
        float(experts_total)
        * float(hidden_width * lax.axis_size("dp"))
        * float(feature_width * lax.axis_size("ffn"))
    )
    clip_limit = jnp.float32(0.5 * math.sqrt(entry_count))
    factor = clip_limit / jnp.maximum(jnp.sqrt(squares), clip_limit)
    down_grad = (weight_grad * factor).astype(jnp.bfloat16)
    return (down_grad, gate_grad, up_grad)


def solution(mesh):
    placed = (
        P("dp", "ffn"),
        P("dp", None),
        P("dp", None),
        P("expert", "ffn", "dp"),
        P("expert", "ffn", "dp"),
        P("expert", "dp", "ffn"),
    )
    return jax.shard_map(
        on_device,
        mesh=mesh,
        in_specs=placed,
        out_specs=(P("expert", "dp", "ffn"), P("expert", "ffn", "dp"), P("expert", "ffn", "dp")),
        check_vma=False,
    )
```

profile of v0, /device:TPU:6, one launch (start us, length us, event | category | flops | bytes accessed | tf_op | source)
XLA Modules:
  0.0 323.1 jit_solution(6122541284965118763)
XLA Ops:
  7.2 0.0 copy-start
  7.2 0.0 copy-start.3
  7.2 0.0 all-gather.5.cloned.1.call-start
  7.2 0.9 copy.13
  8.1 0.1 eq.57
  8.3 0.1 eq.53
  8.4 0.7 broadcast_subtract_fusion
  9.1 0.1 copy.17
  9.2 1.2 reduce-window.6
  10.4 0.1 slice.8
  10.5 0.1 copy.15
  10.7 0.1 copy.16
  10.8 0.1 add_bitcast_fusion
  10.9 0.1 eq.61
  11.0 0.8 copy.18
  11.8 1.1 fusion.9
  12.9 0.1 copy.19
  13.0 0.0 copy-done.3
  13.0 1.0 convolution_convert_fusion.1
  14.1 0.0 all-gather.5.cloned.1.call-update
  14.1 0.0 reduce-scatter.2.cloned.1.call-start
  14.1 100.0 %all-gather.5.cloned.1.call-done = bf16[2,2304,768]{2,1,0:T(8,128)(2,1)} async-done(((bf16[2,72,768]{2,1,0:T(8,128)(2,1)}), bf16[2,2304,768]{2,1,0:T(8,128)(2,1)}) %all-gather.5.cloned.1.call-update) | async-done | bytes 7077904 | tf_op jit(solution)/shard_map/all_gather | solution.py:40
  114.1 6.5 %convolution_convert_fusion = bf16[2,2304,256]{2,1,0:T(8,128)(2,1)} fusion(bf16[2,2304,768]{2,1,0:T(8,128)(2,1)} %all-gather.5.cloned.1.call-done, bf16[2,256,768]{2,1,0:T(8,128)(2,1)S(1)} %copy-done), kind=kOutput, calls=%fused_computation | convolution fusion | flops 1813118976 | bytes 10223616 | tf_op jit(solution)/shard_map/erd,efd->erf/dot_general | solution.py:46
  120.6 0.0 reduce-scatter.2.cloned.1.call-update
  120.7 0.0 all-gather.3.cloned.1.call-start
  120.7 46.1 %reduce-scatter.2.cloned.1.call-done = bf16[2,288,256]{2,1,0:T(8,128)(2,1)} async-done(((bf16[2,2304,256]{2,1,0:T(8,128)(2,1)}), bf16[2,288,256]{2,1,0:T(8,128)(2,1)}) %reduce-scatter.2.cloned.1.call-update) | async-done | bytes 294928 | tf_op jit(solution)/shard_map/reduce_scatter | solution.py:49
  166.8 2.3 fusion.4
  169.2 0.0 all-gather.3.cloned.1.call-update
  169.2 44.0 %all-gather.3.cloned.1.call-done = bf16[2,2304,256]{2,1,0:T(8,128)(2,1)} async-done(((bf16[2,288,256]{2,1,0:T(8,128)(2,1)}), bf16[2,2304,256]{2,1,0:T(8,128)(2,1)}) %all-gather.3.cloned.1.call-update) | async-done | bytes 2359312 | tf_op jit(solution)/shard_map/all_gather | solution.py:58
  213.2 6.5 %multiply_reduce_fusion = (f32[]{:T(128)}, f32[2,256,768]{2,1,0:T(8,128)S(1)}) fusion(bf16[2,2304,256]{2,1,0:T(8,128)(2,1)} %all-gather.3.cloned.1.call-done, bf16[2,2304,768]{2,1,0:T(8,128)(2,1)} %all-gather.5.cloned.1.call-done), kind=kOutput, calls=%fused_computation.2 | convolution fusion | flops 1812725760 | bytes 11010052 | tf_op jit(solution)/shard_map/erf,erd->efd/dot_general | solution.py:56
  219.7 95.1 %psum.7 = f32[]{:T(128)} all-reduce(f32[]{:T(128)} %get-tuple-element.6), channel_id=1, replica_groups=mesh['dp'=32,'expert'=2,'ffn'=8] {'dp','expert','ffn'}, use_global_device_ids=true, to_apply=%region_4.5 | all-reduce | flops 1 | bytes 8 | tf_op jit(solution)/shard_map/psum | solution.py:62
  315.6 1.0 multiply_convert_fusion
  (9 shorter events, 0.1 us)
Async XLA Ops:
  7.2 107.0 %copy-start = (bf16[2,256,768]{2,1,0:T(8,128)(2,1)S(1)}, bf16[2,256,768]{2,1,0:T(8,128)(2,1)}, u32[]{:S(2)}) copy-start(bf16[2,256,768]{2,1,0:T(8,128)(2,1)} %param.11) | copy-start | bytes 2359300
  7.2 5.9 %copy-start.3 = (bf16[128,768]{1,0:T(8,128)(2,1)S(1)}, bf16[128,768]{1,0:T(8,128)(2,1)}, u32[]{:S(2)}) copy-start(bf16[128,768]{1,0:T(8,128)(2,1)} %param.6) | copy-start | bytes 589828
  7.2 106.9 %all-gather.5.cloned.1.call-start = ((), (), s32[]{:S(2)}) async-start(), calls=%async_computation.2 | async-start | bytes 7299072 | tf_op jit(solution)/shard_map/all_gather | solution.py:40
  14.1 152.8 %reduce-scatter.2.cloned.1.call-start = ((), (), s32[]{:S(2)}) async-start(), calls=%async_computation.3 | async-start | bytes 2654208 | tf_op jit(solution)/shard_map/reduce_scatter | solution.py:49
  120.6 46.2 %copy-start.1 = (bf16[2,288,256]{2,1,0:T(8,128)(2,1)S(1)}, bf16[2,288,256]{2,1,0:T(8,128)(2,1)}, u32[]{:S(2)}) copy-start(bf16[2,288,256]{2,1,0:T(8,128)(2,1)} %param.9) | copy-start | bytes 884740
  120.6 46.2 %copy-start.2 = (bf16[2,288,256]{2,1,0:T(8,128)(2,1)S(1)}, bf16[2,288,256]{2,1,0:T(8,128)(2,1)}, u32[]{:S(2)}) copy-start(bf16[2,288,256]{2,1,0:T(8,128)(2,1)} %param.10) | copy-start | bytes 884740
  120.7 92.5 %all-gather.3.cloned.1.call-start = ((), (), s32[]{:S(2)}) async-start(), calls=%async_computation.1 | async-start | bytes 2654208 | tf_op jit(solution)/shard_map/all_gather | solution.py:58
Sparse Core Ops, SparseCore 0:
  14.2 99.8 all-gather.4
  120.8 46.0 reduce-scatter.1
  169.5 43.6 all-gather.2
where the time goes:
time: 326 us; the launch traced here: 323 us
  waiting for transfers between devices  190 us (58%)
  blocking collectives  95.1 us (29%)
  matrix products  15.2 us (5%)
  between operations  14.5 us (4%)
  other arithmetic  5.35 us (2%)
    all_gather x1, waiting for transfers between devices, on_device(): arrived = lax.all_gather(dispatched, 'dp', axis=1, tiled=True)  100 us
    psum x1, blocking collectives, on_device(): lax.psum(jnp.sum(weight_grad * weight_grad), ('dp', 'expert', 'ffn'))  95.1 us
    reduce_scatter x1, waiting for transfers between devices, on_device(): lax.psum_scatter(partial_sums.astype(jnp.bfloat16), 'ffn', scatter_dimens...  46.1 us
    all_gather x1, waiting for transfers between devices, on_device(): lax.all_gather(hidden, 'ffn', axis=1, tiled=True)  44 us
    dot_general x1, matrix products, on_device(): jnp.einsum('erf,erd->efd', lax.all_gather(hidden, 'ffn', axis=1, tiled=Tr...  6.55 us
  transfers between devices with their start and end apart: 3, of which 3 were waited for; matrix products, arithmetic and copies ran while one was open for 0% of the time, Pallas kernels for 0%

commit v1 on v0

v1 whole, which is shorter than its diff:
```python
import math

import jax
import jax.numpy as jnp
from jax import lax
from jax.experimental import pallas as pl
from jax.experimental.pallas import tpu as pltpu
from jax.sharding import PartitionSpec as P

CAP = 72
META = 8


def hidden_kernel(gate_ref, up_ref, hidden_ref):
    gate = gate_ref[...].astype(jnp.float32)
    up = up_ref[...].astype(jnp.float32)
    hidden_ref[0] = (gate * jax.nn.sigmoid(gate) * up).astype(jnp.bfloat16)


def hidden_copies(gate_pre, up_pre, copies):
    return pl.pallas_call(
        hidden_kernel,
        grid=(copies,),
        in_specs=[pl.BlockSpec(gate_pre.shape, lambda i: (0, 0, 0))] * 2,
        out_specs=pl.BlockSpec((1,) + gate_pre.shape, lambda i: (i, 0, 0, 0)),
        out_shape=jax.ShapeDtypeStruct((copies,) + gate_pre.shape, jnp.bfloat16),
        name="hidden_copies",
    )(gate_pre, up_pre)


def gate_up_kernel(grad_ref, gate_ref, up_ref, after_ref, gate_out_ref, up_out_ref):
    gate = gate_ref[0].astype(jnp.float32)
    up = up_ref[0].astype(jnp.float32)
    grad = grad_ref[0].astype(jnp.float32)
    sigmoid_gate = jax.nn.sigmoid(gate)
    gate_out_ref[0] = (grad * up * sigmoid_gate * (1.0 + gate * (1.0 - sigmoid_gate))).astype(jnp.bfloat16)
    up_out_ref[0] = (grad * (gate * sigmoid_gate)).astype(jnp.bfloat16)


def gate_up_grads(own_grad, gate_pre, up_pre, after):
    experts, rows, width = gate_pre.shape
    block = pl.BlockSpec((1, rows, width), lambda i: (i, 0, 0))
    return pl.pallas_call(
        gate_up_kernel,
        grid=(experts,),
        in_specs=[block, block, block, pl.BlockSpec(memory_space=pl.ANY)],
        out_specs=[block, block],
        out_shape=[jax.ShapeDtypeStruct(gate_pre.shape, jnp.bfloat16)] * 2,
        name="gate_up_grads",
    )(own_grad, gate_pre, up_pre, after)


def dispatch_kernel(first_ref, rows_ref, weight_ref, after_ref, placed_ref, partial_ref):
    blocks, halves, padded, _ = rows_ref.shape
    experts_here = weight_ref.shape[0]
    half = padded - META
    tokens = halves * half
    before = lax.broadcasted_iota(jnp.int32, (tokens, tokens), 0)
    after = lax.broadcasted_iota(jnp.int32, (tokens, tokens), 1)
    earlier = (before < after).astype(jnp.bfloat16)
    slot_row = lax.broadcasted_iota(jnp.int32, (CAP, tokens), 0).astype(jnp.float32)
    first = first_ref[0].astype(jnp.float32)
    for block in range(blocks):
        meta = rows_ref[block, 0, half:padded, 0:tokens].astype(jnp.float32)
        first_id, second_id = meta[0:1], meta[1:2]
        first_prob = (meta[2:3] + meta[3:4]) + meta[4:5]
        second_prob = (meta[5:6] + meta[6:7]) + meta[7:8]
        members, probs = [], []
        for expert in range(experts_here):
            one = first_id == first + expert
            two = second_id == first + expert
            members.append(jnp.logical_or(one, two).astype(jnp.float32))
            probs.append(jnp.where(one, first_prob, jnp.where(two, second_prob, 0.0)))
        member = jnp.concatenate(members + [jnp.zeros((8 - experts_here, tokens), jnp.float32)], axis=0)
        slots = jnp.dot(member.astype(jnp.bfloat16), earlier, preferred_element_type=jnp.float32)
        tokens_here = jnp.concatenate([rows_ref[block, part, 0:half, :] for part in range(halves)], axis=0)
        for expert in range(experts_here):
            chosen = jnp.where(slot_row == slots[expert : expert + 1], members[expert], 0.0)
            scale = jnp.sum(chosen * probs[expert], axis=1, keepdims=True)
            picked = jnp.dot(chosen.astype(jnp.bfloat16), tokens_here, preferred_element_type=jnp.float32)
            placed_ref[expert, block * CAP : (block + 1) * CAP, :] = (picked * scale).astype(jnp.bfloat16)
    for expert in range(experts_here):
        partial_ref[expert] = lax.dot_general(
            placed_ref[expert],
            weight_ref[expert],
            (((1,), (1,)), ((), ())),
            preferred_element_type=jnp.float32,
        ).astype(jnp.bfloat16)


def dispatch_and_project(first_expert, gathered, down_weight, after, owners):
    sources, halves, padded, width = gathered.shape
    experts_here, hidden_width, _ = down_weight.shape
    rows = sources * CAP
    per_step = sources // owners
    return pl.pallas_call(
        dispatch_kernel,
        grid_spec=pltpu.PrefetchScalarGridSpec(
            num_scalar_prefetch=1,
            grid=(owners,),
            in_specs=[
                pl.BlockSpec((per_step, halves, padded, width), lambda i, s: (i, 0, 0, 0)),
                pl.BlockSpec((experts_here, hidden_width, width), lambda i, s: (0, 0, 0)),
                pl.BlockSpec(memory_space=pl.ANY),
            ],
            out_specs=[
                pl.BlockSpec((experts_here, per_step * CAP, width), lambda i, s: (0, i, 0)),
                pl.BlockSpec((experts_here, per_step * CAP, hidden_width), lambda i, s: (0, i, 0)),
            ],
        ),
        out_shape=[
            jax.ShapeDtypeStruct((experts_here, rows, width), jnp.bfloat16),
            jax.ShapeDtypeStruct((experts_here, rows, hidden_width), jnp.bfloat16),
        ],
        compiler_params=pltpu.CompilerParams(dimension_semantics=("arbitrary",)),
        name="dispatch_project",
    )(first_expert.reshape(1), gathered, down_weight, after)


def three_pieces(value):
    high = lax.reduce_precision(value, 8, 7)
    rest = value - high
    middle = lax.reduce_precision(rest, 8, 7)
    return high, middle, rest - middle


def total_over_mesh(value):
    row = jnp.full((1, 128), value, jnp.float32)
    for axis in ("dp", "ffn", "expert"):
        size = lax.axis_size(axis)
        copies = jnp.broadcast_to(row, (size, 128))
        if size == 2:
            row = row + lax.ppermute(row, axis, [(0, 1), (1, 0)])
        else:
            row = jnp.sum(lax.all_to_all(copies, axis, 0, 0, tiled=True), axis=0, keepdims=True)
    return row[0, 0]


def on_device(grad_rows, gate_probs, expert_ids, gate_pre, up_pre, down_weight):
    experts_here, rows_here, hidden_width = gate_pre.shape
    tokens_here, feature_width = grad_rows.shape
    cores = lax.axis_size("expert")
    sources = lax.axis_size("dp")
    owners = lax.axis_size("ffn")
    experts_total = experts_here * cores
    core = lax.axis_index("expert")
    half = tokens_here // cores

    pieces = [expert_ids[:, 0].astype(jnp.float32), expert_ids[:, 1].astype(jnp.float32)]
    pieces += list(three_pieces(gate_probs[:, 0])) + list(three_pieces(gate_probs[:, 1]))
    meta = jnp.stack(pieces).astype(jnp.bfloat16)
    meta = jnp.pad(meta, ((0, 0), (0, feature_width - tokens_here)))
    own_rows = lax.dynamic_slice_in_dim(grad_rows, core * half, half, axis=0)
    payload = jnp.concatenate([own_rows, meta], axis=0)
    gathered = lax.all_gather(payload, ("dp", "expert"), axis=0, tiled=False)
    gathered = gathered.reshape(sources, cores, half + META, feature_width)

    spread = hidden_copies(gate_pre, up_pre, owners)
    hidden_all = lax.all_to_all(spread, "ffn", 0, 0, tiled=True)

    arrived, partial_sums = dispatch_and_project(
        core * experts_here, gathered, down_weight, hidden_all, owners
    )
    own_grad = lax.psum_scatter(partial_sums, "ffn", scatter_dimension=1, tiled=True)

    weight_grad = jnp.einsum(
        "zerf,ezrd->efd",
        hidden_all,
        arrived.reshape(experts_here, owners, rows_here, feature_width),
        preferred_element_type=jnp.float32,
    )
    squares = total_over_mesh(jnp.sum(weight_grad * weight_grad))
    entry_count = (
        float(experts_total) * float(hidden_width * sources) * float(feature_width * owners)
    )
    clip_limit = jnp.float32(0.5 * math.sqrt(entry_count))
    factor = clip_limit / jnp.maximum(jnp.sqrt(squares), clip_limit)
    down_grad = (weight_grad * factor).astype(jnp.bfloat16)

    gate_grad, up_grad = gate_up_grads(own_grad, gate_pre, up_pre, down_grad)
    return (down_grad, gate_grad, up_grad)


def solution(mesh):
    placed = (
        P("dp", "ffn"),
        P("dp", None),
        P("dp", None),
        P("expert", "ffn", "dp"),
        P("expert", "ffn", "dp"),
        P("expert", "dp", "ffn"),
    )
    return jax.shard_map(
        on_device,
        mesh=mesh,
        in_specs=placed,
        out_specs=(P("expert", "dp", "ffn"), P("expert", "ffn", "dp"), P("expert", "ffn", "dp")),
        check_vma=False,
    )
```

time: 326 us -> 173 us (0.53)
  waiting for transfers between devices: 190 us -> 79.2 us
  blocking collectives: 95.1 us -> 30 us
  Pallas kernels: 0 us -> 20.5 us
  starting transfers between devices: 0.12 us -> 12.3 us
  matrix products: 15.2 us -> 6.81 us
    all_gather x2 -> x1, waiting for transfers between devices: 144 us -> 20.5 us  [on_device(): gathered = lax.all_gather(payload, ('dp', 'expert'), axis=0, tiled=False)]
    psum x1 -> x0, blocking collectives: 95.1 us -> none  [on_device(): lax.psum(jnp.sum(weight_grad * weight_grad), ('dp', 'expert', 'ffn'))]
    all_to_all x0 -> x1, waiting for transfers between devices: none -> 56.8 us  [on_device(): hidden_all = lax.all_to_all(spread, 'ffn', 0, 0, tiled=True)]
    reduce_scatter x1, waiting for transfers between devices: 46.1 us -> 0.86 us  [on_device(): lax.psum_scatter(partial_sums, 'ffn', scatter_dimension=1, tiled=True)]
    all_to_all x0 -> x2, blocking collectives: none -> 30 us  [total_over_mesh(): lax.all_to_all(copies, axis, 0, 0, tiled=True)]
    pallas_call x0 -> x3, Pallas kernels: none -> 20.5 us  [the longest x1 13.7 us: dispatch_and_project(): pl.pallas_call(dispatch_kernel, grid_spec=pltpu.PrefetchScalarGridSpec(nu...]
    all_to_all x0 -> x1, starting transfers between devices: none -> 10.3 us  [on_device(): hidden_all = lax.all_to_all(spread, 'ffn', 0, 0, tiled=True)]
    dot_general x4 -> x1, matrix products: 15.2 us -> 6.81 us  [on_device(): jnp.einsum('zerf,ezrd->efd', hidden_all, arrived.reshape(experts_here, ow...]
  transfers between devices with their start and end apart: 3 -> 4, of which waited for: 3 -> 4; matrix products, arithmetic and copies ran while one was open for 0% -> 6% of each run, Pallas kernels for 0% -> 3%
where the time goes in v1:
time: 173 us; the launch traced here: 170 us
  waiting for transfers between devices  79.2 us (46%)
  blocking collectives  30 us (17%)
  Pallas kernels  20.5 us (12%)
  between operations  14.2 us (8%)
  starting transfers between devices  12.3 us (7%)
  matrix products  6.81 us (4%)
  other arithmetic  4.62 us (3%)
  local copies, waits for them, and re-layouts  2.36 us (1%)
    all_to_all x1, waiting for transfers between devices, on_device(): hidden_all = lax.all_to_all(spread, 'ffn', 0, 0, tiled=True)  56.8 us
    all_to_all x2, blocking collectives, total_over_mesh(): lax.all_to_all(copies, axis, 0, 0, tiled=True)  30 us
    all_gather x1, waiting for transfers between devices, on_device(): gathered = lax.all_gather(payload, ('dp', 'expert'), axis=0, tiled=False)  20.5 us
    pallas_call x1, Pallas kernels, dispatch_and_project(): pl.pallas_call(dispatch_kernel, grid_spec=pltpu.PrefetchScalarGridSpec(nu...  13.7 us
    all_to_all x1, starting transfers between devices, on_device(): hidden_all = lax.all_to_all(spread, 'ffn', 0, 0, tiled=True)  10.3 us
    dot_general x1, matrix products, on_device(): jnp.einsum('zerf,ezrd->efd', hidden_all, arrived.reshape(experts_here, ow...  6.81 us
    pallas_call x1, Pallas kernels, hidden_copies(): pl.pallas_call(hidden_kernel, grid=(copies,), in_specs=[pl.BlockSpec(gate...  4.64 us
  transfers between devices with their start and end apart: 4, of which 4 were waited for; matrix products, arithmetic and copies ran while one was open for 6% of the time, Pallas kernels for 3%

profile of v1, /device:TPU:6, one launch (start us, length us, event | category | flops | bytes accessed | tf_op | source)
XLA Modules:
  0.0 169.9 jit_solution(12055397452230206233)
XLA Ops:
  7.2 0.0 copy-start
  7.2 0.0 all-gather.3.cloned.1.call-start
  7.2 0.8 convert_bitcast_fusion
  8.0 0.8 fusion.7
  8.8 0.0 copy-done
  8.8 0.7 fusion.5
  9.5 0.0 all-gather.3.cloned.1.call-update
  9.5 4.6 %hidden_copies.1 = bf16[8,2,288,256]{3,2,1,0:T(8,128)(2,1)} custom-call(bf16[2,288,256]{2,1,0:T(8,128)(2,1)} %gate_ref.3, bf16[2,288,256]{2,1,0:T(8,128)(2,1)} %up_ref.3), custom_call_target="tpu_custom_call" | custom-call | tf_op jit(solution)/shard_map/hidden_copies/pallas_call | solution.py:21
  14.1 10.3 %all-to-all-start = ((bf16[8,2,288,256]{3,2,1,0:T(8,128)(2,1)}), bf16[8,2,288,256]{3,2,1,0:T(8,128)(2,1)S(1)}, u32[]{:S(2)}, u32[]{:S(2)}) async-start(bf16[8,2,288,256]{3,2,1,0:T(8,128)(2,1)} %hidden_copies.1), calls=%async_computation | async-start | bytes 4718592 | tf_op jit(solution)/shard_map/all_to_all | solution.py:159
  24.4 0.0 reduce-scatter.2.cloned.1.call-start
  24.5 56.8 %all-to-all-done.after_ref = bf16[8,2,288,256]{3,2,1,0:T(8,128)(2,1)S(1)} async-done(((bf16[8,2,288,256]{3,2,1,0:T(8,128)(2,1)}), bf16[8,2,288,256]{3,2,1,0:T(8,128)(2,1)S(1)}, u32[]{:S(2)}, u32[]{:S(2)}) %all-to-all-start) | async-done | bytes 2359328 | tf_op jit(solution)/shard_map/all_to_all | solution.py:159
  81.3 0.0 copy-start.1
  81.3 20.5 %all-gather.3.cloned.1.call-done = bf16[4608,768]{1,0:T(8,128)(2,1)} async-done(((bf16[72,768]{1,0:T(8,128)(2,1)}), bf16[4608,768]{1,0:T(8,128)(2,1)}) %all-gather.3.cloned.1.call-update) | async-done | bytes 7077904 | tf_op jit(solution)/shard_map/all_gather | solution.py:155
  101.7 0.0 copy-done.1
  101.7 13.7 %dispatch_project.1 = (bf16[2,2304,768]{2,1,0:T(8,128)(2,1)}, bf16[2,2304,256]{2,1,0:T(8,128)(2,1)}) custom-call(s32[1]{0:T(128)} %bitcast.first_ref, bf16[32,2,72,768]{3,2,1,0:T(8,128)(2,1)} %bitcast.35, bf16[2,256,768]{2,1,0:T(8,128)(2,1)} %weight_ref.1, bf16[8,2,288,256]{3,2,1,0:T(8,128)(2,1)} %copy-done.1), custom_call_target="tpu_custom_call" | custom-call | tf_op jit(solution)/shard_map/dispatch_project/pallas_call | solution.py:96
  115.5 0.0 copy-start.2
  115.5 0.0 reduce-scatter.2.cloned.1.call-update
  115.5 1.6 copy-done.2
  117.1 6.8 %fusion.2 = (f32[]{:T(128)}, f32[2,256,768,1]{2,1,0,3:T(8,128)}) fusion(bf16[8,2,288,256]{3,2,1,0:T(8,128)(2,1)S(1)} %copy-done.2, bf16[2,8,288,768]{3,2,1,0:T(8,128)(2,1)} %bitcast.39), kind=kOutput, calls=%fused_computation.4 | convolution fusion | flops 1812725760 | bytes 11010052 | tf_op jit(solution)/shard_map/zerf,ezrd->efd/dot_general | solution.py:166
  123.9 0.7 broadcast_in_dim_broadcast_in_dim.3
  124.6 15.1 %all_to_all.17 = f32[32,1,128]{2,1,0:T(1,128)S(1)} all-to-all(f32[32,1,128]{2,1,0:T(1,128)S(1)} %broadcast_in_dim_broadcast_in_dim.3), channel_id=1, replica_groups=mesh['dp'=32,'expert'=2,'ffn'=8] {'dp'}, dimensions={0} | all-to-all | bytes 32768 | tf_op jit(solution)/shard_map/all_to_all | solution.py:135
  139.7 14.8 %all_to_all.18 = f32[8,1,128]{2,1,0:T(1,128)S(1)} all-to-all(f32[8,1,128]{2,1,0:T(1,128)S(1)} %broadcast_in_dim.4), channel_id=1, replica_groups=mesh['dp'=32,'expert'=2,'ffn'=8] {'ffn'}, dimensions={0} | all-to-all | bytes 8192 | tf_op jit(solution)/shard_map/all_to_all | solution.py:135
  154.6 1.9 %collective-permute-start = (f32[1,128]{1,0:T(1,128)S(1)}, f32[1,128]{1,0:T(1,128)S(1)}, u32[]{:S(2)}, u32[]{:S(2)}) collective-permute-start(f32[1,128]{1,0:T(1,128)S(1)} %bitcast.38), channel_id=1, source_target_pairs={{0,8},{8,0},{1,9},{9,1},{2,10},{10,2},{3,11},{11,3},{4,12},{12,4},... | collective-permute-start | bytes 1544 | tf_op jit(solution)/shard_map/ppermute | solution.py:133
  156.5 1.1 collective-permute-done
  157.7 2.4 %fusion.3.after_ref = bf16[2,256,768]{2,1,0:T(8,128)(2,1)} fusion(f32[2,256,768,1]{2,1,0,3:T(8,128)} %get-tuple-element.20, f32[]{:T(128)} %bitcast.11), kind=kLoop, calls=%fused_computation.5 | loop fusion | flops 786432 | bytes 2359300 | tf_op jit(solution)/shard_map/convert_element_type | solution.py:178
  160.1 0.9 reduce-scatter.2.cloned.1.call-done.grad_ref
  161.0 2.1 %gate_up_grads.1 = (bf16[2,288,256]{2,1,0:T(8,128)(2,1)}, bf16[2,288,256]{2,1,0:T(8,128)(2,1)}) custom-call(bf16[2,288,256]{2,1,0:T(8,128)(2,1)} %reduce-scatter.2.cloned.1.call-done.grad_ref, bf16[2,288,256]{2,1,0:T(8,128)(2,1)} %gate_ref.3, bf16[2,288,256]{2,1,0:T(8,128)(2,1)} %up_ref.3, bf16[2,256,768]{2,1,0:T(8,128)(2,1)} %fusion.3.after_ref), custom_call_target="tpu_custom_call" | custom-call | tf_op jit(solution)/shard_map/gate_up_grads/pallas_call | solution.py:43
  (6 shorter events, 0.1 us)
Async XLA Ops:
  7.2 1.6 copy-start
  7.2 94.6 %all-gather.3.cloned.1.call-start = ((), (), s32[]{:S(2)}) async-start(), calls=%async_computation.5 | async-start | bytes 7188480 | tf_op jit(solution)/shard_map/all_gather | solution.py:155
  14.1 67.2 %all-to-all-start = ((bf16[8,2,288,256]{3,2,1,0:T(8,128)(2,1)}), bf16[8,2,288,256]{3,2,1,0:T(8,128)(2,1)S(1)}, u32[]{:S(2)}, u32[]{:S(2)}) async-start(bf16[8,2,288,256]{3,2,1,0:T(8,128)(2,1)} %hidden_copies.1), calls=%async_computation | async-start | bytes 4718592 | tf_op jit(solution)/shard_map/all_to_all | solution.py:159
  24.4 136.6 %reduce-scatter.2.cloned.1.call-start = ((), (), s32[]{:S(2)}) async-start(), calls=%async_computation.4 | async-start | bytes 2654208 | tf_op jit(solution)/shard_map/reduce_scatter | solution.py:164
  81.3 20.5 %copy-start.1 = (bf16[8,2,288,256]{3,2,1,0:T(8,128)(2,1)}, bf16[8,2,288,256]{3,2,1,0:T(8,128)(2,1)S(1)}, u32[]{:S(2)}) copy-start(bf16[8,2,288,256]{3,2,1,0:T(8,128)(2,1)S(1)} %all-to-all-done.after_ref) | copy-start | bytes 7077892
  115.5 1.7 copy-start.2
  154.6 3.0 %collective-permute-start = (f32[1,128]{1,0:T(1,128)S(1)}, f32[1,128]{1,0:T(1,128)S(1)}, u32[]{:S(2)}, u32[]{:S(2)}) collective-permute-start(f32[1,128]{1,0:T(1,128)S(1)} %bitcast.38), channel_id=1, source_target_pairs={{0,8},{8,0},{1,9},{9,1},{2,10},{10,2},{3,11},{11,3},{4,12},{12,4},... | collective-permute-start | bytes 1544 | tf_op jit(solution)/shard_map/ppermute | solution.py:133
Sparse Core Ops, SparseCore 0:
  11.9 89.8 all-gather.2
  115.6 45.3 reduce-scatter.1

commit v2 on v1

v2 whole, which is shorter than its diff:
```python
import math

import jax
import jax.numpy as jnp
from jax import lax
from jax.experimental import pallas as pl
from jax.experimental.pallas import tpu as pltpu
from jax.sharding import Mesh
from jax.sharding import PartitionSpec as P

CAP = 72
META = 8
X_CHIPS = 4


def hidden_kernel(gate_ref, up_ref, hidden_ref):
    gate = gate_ref[...].astype(jnp.float32)
    up = up_ref[...].astype(jnp.float32)
    hidden_ref[...] = (gate * jax.nn.sigmoid(gate) * up).astype(jnp.bfloat16)


def hidden_rows(gate_pre, up_pre):
    experts, rows, width = gate_pre.shape
    block = pl.BlockSpec((1, rows, width), lambda i: (i, 0, 0))
    return pl.pallas_call(
        hidden_kernel,
        grid=(experts,),
        in_specs=[block, block],
        out_specs=block,
        out_shape=jax.ShapeDtypeStruct(gate_pre.shape, jnp.bfloat16),
        name="hidden_rows",
    )(gate_pre, up_pre)


def gate_up_kernel(grad_ref, gate_ref, up_ref, after_ref, gate_out_ref, up_out_ref):
    gate = gate_ref[0].astype(jnp.float32)
    up = up_ref[0].astype(jnp.float32)
    grad = grad_ref[0].astype(jnp.float32)
    sigmoid_gate = jax.nn.sigmoid(gate)
    gate_out_ref[0] = (grad * up * sigmoid_gate * (1.0 + gate * (1.0 - sigmoid_gate))).astype(jnp.bfloat16)
    up_out_ref[0] = (grad * (gate * sigmoid_gate)).astype(jnp.bfloat16)


def gate_up_grads(own_grad, gate_pre, up_pre, after):
    experts, rows, width = gate_pre.shape
    block = pl.BlockSpec((1, rows, width), lambda i: (i, 0, 0))
    return pl.pallas_call(
        gate_up_kernel,
        grid=(experts,),
        in_specs=[block, block, block, pl.BlockSpec(memory_space=pl.ANY)],
        out_specs=[block, block],
        out_shape=[jax.ShapeDtypeStruct(gate_pre.shape, jnp.bfloat16)] * 2,
        name="gate_up_grads",
    )(own_grad, gate_pre, up_pre, after)


def dispatch_kernel(place_ref, own_ref, other_ref, weight_ref, *refs):
    placed_ref, partial_ref = refs[-2:]
    blocks, padded, _ = own_ref.shape
    experts_here = weight_ref.shape[0]
    half = padded - META
    tokens = 2 * half
    before = lax.broadcasted_iota(jnp.int32, (tokens, tokens), 0)
    after = lax.broadcasted_iota(jnp.int32, (tokens, tokens), 1)
    earlier = (before < after).astype(jnp.bfloat16)
    slot_row = lax.broadcasted_iota(jnp.int32, (CAP, tokens), 0).astype(jnp.float32)
    core = place_ref[1]
    first = (core * experts_here).astype(jnp.float32)
    for block in range(blocks):
        meta = own_ref[block, half:padded, 0:tokens].astype(jnp.float32)
        first_id, second_id = meta[0:1], meta[1:2]
        first_prob = (meta[2:3] + meta[3:4]) + meta[4:5]
        second_prob = (meta[5:6] + meta[6:7]) + meta[7:8]
        members, probs = [], []
        for expert in range(experts_here):
            one = first_id == first + expert
            two = second_id == first + expert
            members.append(jnp.logical_or(one, two).astype(jnp.float32))
            probs.append(jnp.where(one, first_prob, jnp.where(two, second_prob, 0.0)))
        filler = [jnp.zeros((8 - experts_here, tokens), jnp.float32)]
        member = jnp.concatenate(members + filler, axis=0)
        slots = jnp.dot(member.astype(jnp.bfloat16), earlier, preferred_element_type=jnp.float32)
        slots = jnp.where(member > 0.0, slots, -1.0)
        prob = jnp.concatenate(probs + filler, axis=0)
        slots = jnp.where(core == 1, pltpu.roll(slots, half, 1), slots)
        prob = jnp.where(core == 1, pltpu.roll(prob, half, 1), prob)
        tokens_here = jnp.concatenate([own_ref[block, 0:half, :], other_ref[block, 0:half, :]], axis=0)
        chosen, scales = [], []
        for expert in range(experts_here):
            match = (slot_row == slots[expert : expert + 1]).astype(jnp.float32)
            chosen.append(match)
            scales.append(jnp.sum(match * prob[expert : expert + 1], axis=1, keepdims=True))
        picked = jnp.dot(
            jnp.concatenate(chosen, axis=0).astype(jnp.bfloat16),
            tokens_here,
            preferred_element_type=jnp.float32,
        )
        scaled = (picked * jnp.concatenate(scales, axis=0)).astype(jnp.bfloat16)
        for expert in range(experts_here):
            placed_ref[expert, block * CAP : (block + 1) * CAP, :] = scaled[expert * CAP : (expert + 1) * CAP]
    for expert in range(experts_here):
        partial_ref[expert] = lax.dot_general(
            placed_ref[expert],
            weight_ref[expert],
            (((1,), (1,)), ((), ())),
            preferred_element_type=jnp.float32,
        ).astype(jnp.bfloat16)


def dispatch_and_project(plane, core, own_half, other_half, down_weight, rows, buffers):
    sources, padded, width = own_half.shape
    experts_here, hidden_width, _ = down_weight.shape
    steps = 2
    per_step = sources // steps
    half_block = pl.BlockSpec((per_step, padded, width), lambda i, s: (i, 0, 0))
    anywhere = [pl.BlockSpec(memory_space=pl.ANY)] * len(buffers)
    return pl.pallas_call(
        dispatch_kernel,
        grid_spec=pltpu.PrefetchScalarGridSpec(
            num_scalar_prefetch=1,
            grid=(steps,),
            in_specs=[
                half_block,
                half_block,
                pl.BlockSpec((experts_here, hidden_width, width), lambda i, s: (0, 0, 0)),
            ]
            + anywhere,
            out_specs=[
                pl.BlockSpec((experts_here, per_step * CAP, width), lambda i, s: (0, s[0] * steps + i, 0)),
                pl.BlockSpec((experts_here, per_step * CAP, hidden_width), lambda i, s: (0, s[0] * steps + i, 0)),
            ],
        ),
        out_shape=[
            jax.ShapeDtypeStruct((experts_here, rows, width), jnp.bfloat16),
            jax.ShapeDtypeStruct((experts_here, rows, hidden_width), jnp.bfloat16),
        ],
        input_output_aliases={4 + i: i for i in range(len(buffers))},
        compiler_params=pltpu.CompilerParams(dimension_semantics=("arbitrary",)),
        name="dispatch_project",
    )(jnp.stack([plane, core]).astype(jnp.int32), own_half, other_half, down_weight, *buffers)


def three_pieces(value):
    high = lax.reduce_precision(value, 8, 7)
    rest = value - high
    middle = lax.reduce_precision(rest, 8, 7)
    return high, middle, rest - middle


def total_over_mesh(value):
    row = jnp.full((1, 128), value, jnp.float32)
    for axis in (("x", "y"), "ffn"):
        copies = jnp.broadcast_to(row, (lax.axis_size(axis), 128))
        row = jnp.sum(lax.all_to_all(copies, axis, 0, 0, tiled=True), axis=0, keepdims=True)
    row = row + swap_cores(row)
    return row[0, 0]


def swap_cores(value):
    return lax.ppermute(value, "expert", [(0, 1), (1, 0)])


def along_x(value):
    size = lax.axis_size("x")
    pairs = []
    for place in range(size):
        pairs.append((place * 2, (place + 1) % size * 2))
        pairs.append((place * 2 + 1, (place - 1) % size * 2 + 1))
    return lax.ppermute(value, ("x", "expert"), pairs)


def on_device(grad_rows, gate_probs, expert_ids, gate_pre, up_pre, down_weight):
    experts_here, rows_here, hidden_width = gate_pre.shape
    tokens_here, feature_width = grad_rows.shape
    cores = lax.axis_size("expert")
    planes = lax.axis_size("x")
    lines = lax.axis_size("y")
    sources = planes * lines
    owners = lax.axis_size("ffn")
    experts_total = experts_here * cores
    core = lax.axis_index("expert")
    plane = lax.axis_index("x")
    half = tokens_here // cores
    rows = rows_here * owners

    pieces = [expert_ids[:, 0].astype(jnp.float32), expert_ids[:, 1].astype(jnp.float32)]
    pieces += list(three_pieces(gate_probs[:, 0])) + list(three_pieces(gate_probs[:, 1]))
    meta = jnp.stack(pieces).astype(jnp.bfloat16)
    meta = jnp.pad(meta, ((0, 0), (0, feature_width - tokens_here)))
    own_rows = lax.dynamic_slice_in_dim(grad_rows, core * half, half, axis=0)
    payload = jnp.concatenate([own_rows, meta], axis=0)
    near = lax.all_to_all(
        jnp.broadcast_to(payload[None], (lines,) + payload.shape), "y", 0, 0, tiled=True
    )

    hidden_all = lax.all_gather(hidden_rows(gate_pre, up_pre), "ffn", axis=1, tiled=True)

    side_own = along_x(near)
    near_other = swap_cores(near)
    side_other = along_x(near_other)
    far_own = along_x(side_own)
    beyond_other = swap_cores(side_own)
    beyond_own = swap_cores(side_other)

    def project(offset, own_half, other_half, buffers):
        return dispatch_and_project(
            (plane + offset) % planes, core, own_half, other_half, down_weight, rows, buffers
        )

    buffers = project(0, near, near_other, ())
    buffers = project(planes - 1 + 2 * core, side_own, side_other, buffers)
    far_own, buffers = lax.optimization_barrier((far_own, buffers))
    far_other = swap_cores(far_own)
    buffers = project(1 + planes - 2 * core, beyond_own, beyond_other, buffers)
    buffers = project(2, far_own, far_other, buffers)
    arrived, partial_sums = buffers
    own_grad = lax.psum_scatter(partial_sums, "ffn", scatter_dimension=1, tiled=True)

    weight_grad = jnp.einsum(
        "erf,erd->efd",
        hidden_all,
        arrived,
        preferred_element_type=jnp.float32,
    )
    squares = total_over_mesh(jnp.sum(weight_grad * weight_grad))
    entry_count = (
        float(experts_total) * float(hidden_width * sources) * float(feature_width * owners)
    )
    clip_limit = jnp.float32(0.5 * math.sqrt(entry_count))
    factor = clip_limit / jnp.maximum(jnp.sqrt(squares), clip_limit)
    down_grad = (weight_grad * factor).astype(jnp.bfloat16)

    gate_grad, up_grad = gate_up_grads(own_grad, gate_pre, up_pre, down_grad)
    return (down_grad, gate_grad, up_grad)


def solution(mesh):
    fine = Mesh(mesh.devices.reshape((X_CHIPS, -1) + mesh.devices.shape[1:]), ("x", "y", "expert", "ffn"))
    spread = ("x", "y")
    placed = (
        P(spread, "ffn"),
        P(spread, None),
        P(spread, None),
        P("expert", "ffn", spread),
        P("expert", "ffn", spread),
        P("expert", spread, "ffn"),
    )
    return jax.shard_map(
        on_device,
        mesh=fine,
        in_specs=placed,
        out_specs=(P("expert", spread, "ffn"), P("expert", "ffn", spread), P("expert", "ffn", spread)),
        check_vma=False,
    )
```

time: 173 us -> 152 us (0.88); the launches traced: 170 us -> 152 us
  waiting for transfers between devices: 79.2 us -> 37.7 us
  starting transfers between devices: 12.3 us -> 26.6 us
  Pallas kernels: 20.5 us -> 28.2 us
    all_to_all x1, waiting for transfers between devices: 56.8 us -> 23.2 us  [on_device(): lax.all_to_all(jnp.broadcast_to(payload[None], (lines,) + payload.shape),...]
    all_gather x1, waiting for transfers between devices: 20.5 us -> 0.02 us  [on_device(): lax.all_gather(hidden_rows(gate_pre, up_pre), 'ffn', axis=1, tiled=True)]
    ppermute x1 -> x8, starting transfers between devices: 1.91 us -> 19.4 us  [the longest x5 10.1 us: swap_cores(): return lax.ppermute(value, 'expert', [(0, 1), (1, 0)])]
    pallas_call x1 -> x4, Pallas kernels: 13.7 us -> 24.3 us  [dispatch_and_project(): pl.pallas_call(dispatch_kernel, grid_spec=pltpu.PrefetchScalarGridSpec(nu...]
    ppermute x1 -> x8, waiting for transfers between devices: 1.09 us -> 10.3 us  [the longest x3 9.13 us: along_x(): return lax.ppermute(value, ('x', 'expert'), pairs)]
    reduce_scatter x1, waiting for transfers between devices: 0.86 us -> 4.12 us  [on_device(): lax.psum_scatter(partial_sums, 'ffn', scatter_dimension=1, tiled=True)]
    all_to_all x1, starting transfers between devices: 10.3 us -> 7.1 us  [on_device(): lax.all_to_all(jnp.broadcast_to(payload[None], (lines,) + payload.shape),...]
    pallas_call x1, Pallas kernels: 4.64 us -> 1.87 us  [hidden_rows(): pl.pallas_call(hidden_kernel, grid=(experts,), in_specs=[block, block], o...]
  transfers between devices with their start and end apart: 4 -> 11, of which waited for: 4 -> 5; matrix products, arithmetic and copies ran while one was open for 6% -> 7% of each run, Pallas kernels for 3% -> 17%
where the time goes in v2:
time: 152 us
  waiting for transfers between devices  37.7 us (25%)
  blocking collectives  30.7 us (20%)
  Pallas kernels  28.2 us (19%)
  starting transfers between devices  26.6 us (18%)
  between operations  14.4 us (9%)
  matrix products  6.55 us (4%)
  other arithmetic  4.86 us (3%)
  local copies, waits for them, and re-layouts  2.62 us (2%)
    all_to_all x2, blocking collectives, total_over_mesh(): lax.all_to_all(copies, axis, 0, 0, tiled=True)  30.7 us
    pallas_call x4, Pallas kernels, dispatch_and_project(): pl.pallas_call(dispatch_kernel, grid_spec=pltpu.PrefetchScalarGridSpec(nu...  24.3 us
    all_to_all x1, waiting for transfers between devices, on_device(): lax.all_to_all(jnp.broadcast_to(payload[None], (lines,) + payload.shape),...  23.2 us
    ppermute x5, starting transfers between devices, swap_cores(): return lax.ppermute(value, 'expert', [(0, 1), (1, 0)])  10.1 us
    ppermute x3, starting transfers between devices, along_x(): return lax.ppermute(value, ('x', 'expert'), pairs)  9.34 us
    ppermute x3, waiting for transfers between devices, along_x(): return lax.ppermute(value, ('x', 'expert'), pairs)  9.13 us
    all_to_all x1, starting transfers between devices, on_device(): lax.all_to_all(jnp.broadcast_to(payload[None], (lines,) + payload.shape),...  7.1 us
    dot_general x1, matrix products, on_device(): jnp.einsum('erf,erd->efd', hidden_all, arrived, preferred_element_type=jn...  6.55 us
  transfers between devices with their start and end apart: 11, of which 5 were waited for; matrix products, arithmetic and copies ran while one was open for 7% of the time, Pallas kernels for 17%

profile of v2, /device:TPU:6, one launch (start us, length us, event | category | flops | bytes accessed | tf_op | source)
XLA Modules:
  0.0 151.6 jit_solution(10384564855910891367)
XLA Ops:
  7.2 0.8 fusion.3
  8.0 0.8 convert_bitcast_fusion
  8.8 1.0 broadcast_in_dim.6
  9.7 7.1 %all-to-all-start = ((bf16[8,72,768]{2,1,0:T(8,128)(2,1)}), bf16[8,72,768]{2,1,0:T(8,128)(2,1)S(1)}, u32[]{:S(2)}, u32[]{:S(2)}) async-start(bf16[8,72,768]{2,1,0:T(8,128)(2,1)} %broadcast_in_dim.6), calls=%async_computation | async-start | bytes 1769472 | tf_op jit(solution)/shard_map/all_to_all | solution.py:192
  16.9 1.9 %hidden_rows.1 = bf16[2,288,256]{2,1,0:T(8,128)(2,1)} custom-call(bf16[2,288,256]{2,1,0:T(8,128)(2,1)} %gate_ref.3, bf16[2,288,256]{2,1,0:T(8,128)(2,1)} %up_ref.3), custom_call_target="tpu_custom_call" | custom-call | tf_op jit(solution)/shard_map/hidden_rows/pallas_call | solution.py:25
  18.8 23.2 %all-to-all-done.own_ref = bf16[8,72,768]{2,1,0:T(8,128)(2,1)S(1)} async-done(((bf16[8,72,768]{2,1,0:T(8,128)(2,1)}), bf16[8,72,768]{2,1,0:T(8,128)(2,1)S(1)}, u32[]{:S(2)}, u32[]{:S(2)}) %all-to-all-start) | async-done | bytes 884768 | tf_op jit(solution)/shard_map/all_to_all | solution.py:192
  42.1 1.9 %collective-permute-start.2 = (bf16[8,72,768]{2,1,0:T(8,128)(2,1)S(1)}, bf16[8,72,768]{2,1,0:T(8,128)(2,1)}, u32[]{:S(2)}, u32[]{:S(2)}) collective-permute-start(bf16[8,72,768]{2,1,0:T(8,128)(2,1)S(1)} %all-to-all-done.own_ref), channel_id=1, source_target_pairs={{0,8},{8,0},{1,9},{9,1},{2,10},{10,2},{3,11},{11,3},{4,12},{12,4},... | collective-permute-start | bytes 2654216 | tf_op jit(solution)/shard_map/ppermute | solution.py:160
  44.0 2.4 %collective-permute-start = (bf16[8,72,768]{2,1,0:T(8,128)(2,1)S(1)}, bf16[8,72,768]{2,1,0:T(8,128)(2,1)S(1)}, u32[]{:S(2)}, u32[]{:S(2)}) collective-permute-start(bf16[8,72,768]{2,1,0:T(8,128)(2,1)S(1)} %all-to-all-done.own_ref), channel_id=1, source_target_pairs={{0,128},{8,392},{128,256},{136,8},{256,384},{264,136},{384,0},{392... | collective-permute-start | bytes 2654216 | tf_op jit(solution)/shard_map/ppermute | solution.py:169
  46.5 3.3 %collective-permute-start.3 = (bf16[8,72,768]{2,1,0:T(8,128)(2,1)}, bf16[8,72,768]{2,1,0:T(8,128)(2,1)}, u32[]{:S(2)}, u32[]{:S(2)}) collective-permute-start(bf16[8,72,768]{2,1,0:T(8,128)(2,1)} %collective-permute-done.2.other_ref), channel_id=1, source_target_pairs={{0,128},{8,392},{128,256},{136,8},{256,384},{264,136},{384,0},{392... | collective-permute-start | bytes 2654216 | tf_op jit(solution)/shard_map/ppermute | solution.py:169
  49.8 9.1 %collective-permute-done.own_ref = bf16[8,72,768]{2,1,0:T(8,128)(2,1)S(1)} collective-permute-done((bf16[8,72,768]{2,1,0:T(8,128)(2,1)S(1)}, bf16[8,72,768]{2,1,0:T(8,128)(2,1)S(1)}, u32[]{:S(2)}, u32[]{:S(2)}) %collective-permute-start) | collective-permute-done | bytes 884768 | tf_op jit(solution)/shard_map/ppermute | solution.py:169
  58.9 3.6 %collective-permute-start.1 = (bf16[8,72,768]{2,1,0:T(8,128)(2,1)S(1)}, bf16[8,72,768]{2,1,0:T(8,128)(2,1)S(1)}, u32[]{:S(2)}, u32[]{:S(2)}) collective-permute-start(bf16[8,72,768]{2,1,0:T(8,128)(2,1)S(1)} %collective-permute-done.own_ref), channel_id=1, source_target_pairs={{0,128},{8,392},{128,256},{136,8},{256,384},{264,136},{384,0},{392... | collective-permute-start | bytes 2654216 | tf_op jit(solution)/shard_map/ppermute | solution.py:169
  62.6 0.6 pad_add_fusion.2.place_ref
  63.2 0.6 pad_add_fusion.1.place_ref
  63.7 1.9 %collective-permute-start.6 = (bf16[8,72,768]{2,1,0:T(8,128)(2,1)S(1)}, bf16[8,72,768]{2,1,0:T(8,128)(2,1)}, u32[]{:S(2)}, u32[]{:S(2)}) collective-permute-start(bf16[8,72,768]{2,1,0:T(8,128)(2,1)S(1)} %collective-permute-done.own_ref), channel_id=1, source_target_pairs={{0,8},{8,0},{1,9},{9,1},{2,10},{10,2},{3,11},{11,3},{4,12},{12,4},... | collective-permute-start | bytes 2654216 | tf_op jit(solution)/shard_map/ppermute | solution.py:160
  65.7 6.1 %dispatch_project.4 = (bf16[2,2304,768]{2,1,0:T(8,128)(2,1)}, bf16[2,2304,256]{2,1,0:T(8,128)(2,1)}) custom-call(s32[2]{0:T(128)} %pad_add_fusion.2.place_ref, bf16[8,72,768]{2,1,0:T(8,128)(2,1)} %copy-done.1, bf16[8,72,768]{2,1,0:T(8,128)(2,1)} %collective-permute-done.2.other_ref, bf16[2,256,768]{2,1,0:T(8,128)(2,1)} %weight_ref.7), custom_call_target="tpu_custom_call" | custom-call | tf_op jit(solution)/shard_map/dispatch_project/pallas_call | solution.py:117
  71.8 2.4 %collective-permute-start.5 = (bf16[8,72,768]{2,1,0:T(8,128)(2,1)}, bf16[8,72,768]{2,1,0:T(8,128)(2,1)S(1)}, u32[]{:S(2)}, u32[]{:S(2)}) collective-permute-start(bf16[8,72,768]{2,1,0:T(8,128)(2,1)} %collective-permute-done.3.other_ref), channel_id=1, source_target_pairs={{0,8},{8,0},{1,9},{9,1},{2,10},{10,2},{3,11},{11,3},{4,12},{12,4},... | collective-permute-start | bytes 2654216 | tf_op jit(solution)/shard_map/ppermute | solution.py:160
  74.2 6.0 %dispatch_project.5 = (bf16[2,2304,768]{2,1,0:T(8,128)(2,1)}, bf16[2,2304,256]{2,1,0:T(8,128)(2,1)}) custom-call(s32[2]{0:T(128)} %pad_add_fusion.1.place_ref, bf16[8,72,768]{2,1,0:T(8,128)(2,1)} %copy-done.3, bf16[8,72,768]{2,1,0:T(8,128)(2,1)} %collective-permute-done.3.other_ref, ...), custom_call_target="tpu_custom_call", output_to_operand_aliasing={{0}: (4, {}), {1}: (5, {})} | custom-call | tf_op jit(solution)/shard_map/dispatch_project/pallas_call | solution.py:117
  80.2 1.9 %collective-permute-start.4 = (bf16[8,72,768]{2,1,0:T(8,128)(2,1)S(1)}, bf16[8,72,768]{2,1,0:T(8,128)(2,1)}, u32[]{:S(2)}, u32[]{:S(2)}) collective-permute-start(bf16[8,72,768]{2,1,0:T(8,128)(2,1)S(1)} %collective-permute-done.1.own_ref), channel_id=1, source_target_pairs={{0,8},{8,0},{1,9},{9,1},{2,10},{10,2},{3,11},{11,3},{4,12},{12,4},... | collective-permute-start | bytes 2654216 | tf_op jit(solution)/shard_map/ppermute | solution.py:160
  82.2 0.6 pad_add_fusion.3.place_ref
  82.8 0.6 pad_add_fusion.place_ref
  83.4 0.9 copy-done.4
  84.3 6.0 %dispatch_project.6 = (bf16[2,2304,768]{2,1,0:T(8,128)(2,1)}, bf16[2,2304,256]{2,1,0:T(8,128)(2,1)}) custom-call(s32[2]{0:T(128)} %pad_add_fusion.3.place_ref, bf16[8,72,768]{2,1,0:T(8,128)(2,1)} %copy-done.4, bf16[8,72,768]{2,1,0:T(8,128)(2,1)} %collective-permute-done.6.other_ref, ...), custom_call_target="tpu_custom_call", output_to_operand_aliasing={{0}: (4, {}), {1}: (5, {})} | custom-call | tf_op jit(solution)/shard_map/dispatch_project/pallas_call | solution.py:117
  90.3 6.1 %dispatch_project.7 = (bf16[2,2304,768]{2,1,0:T(8,128)(2,1)}, bf16[2,2304,256]{2,1,0:T(8,128)(2,1)}) custom-call(s32[2]{0:T(128)} %pad_add_fusion.place_ref, bf16[8,72,768]{2,1,0:T(8,128)(2,1)} %copy-done.2, bf16[8,72,768]{2,1,0:T(8,128)(2,1)} %collective-permute-done.4.other_ref, ...), custom_call_target="tpu_custom_call", output_to_operand_aliasing={{0}: (4, {}), {1}: (5, {})} | custom-call | tf_op jit(solution)/shard_map/dispatch_project/pallas_call | solution.py:117
  96.5 6.5 %multiply_reduce_fusion = (f32[]{:T(128)}, f32[2,256,768]{2,1,0:T(8,128)S(1)}) fusion(bf16[2,2304,256]{2,1,0:T(8,128)(2,1)} %all-gather.2.cloned.1.call-done, bf16[2,2304,768]{2,1,0:T(8,128)(2,1)} %get-tuple-element.25), kind=kOutput, calls=%fused_computation.1 | convolution fusion | flops 1812725760 | bytes 11010052 | tf_op jit(solution)/shard_map/erf,erd->efd/dot_general | solution.py:219
  103.0 0.7 broadcast_in_dim_broadcast_in_dim.3
  103.7 12.8 %all_to_all.17 = f32[32,1,128]{2,1,0:T(1,128)S(1)} all-to-all(f32[32,1,128]{2,1,0:T(1,128)S(1)} %broadcast_in_dim_broadcast_in_dim.3), channel_id=1, replica_groups=mesh['x'=4,'y'=8,'expert'=2,'ffn'=8] {'x','y'}, dimensions={0} | all-to-all | bytes 32768 | tf_op jit(solution)/shard_map/all_to_all | solution.py:154
  116.5 17.9 %all_to_all.18 = f32[8,1,128]{2,1,0:T(1,128)S(1)} all-to-all(f32[8,1,128]{2,1,0:T(1,128)S(1)} %broadcast_in_dim.7), channel_id=1, replica_groups=mesh['x'=4,'y'=8,'expert'=2,'ffn'=8] {'ffn'}, dimensions={0} | all-to-all | bytes 8192 | tf_op jit(solution)/shard_map/all_to_all | solution.py:154
  134.4 1.9 %collective-permute-start.7 = (f32[1,128]{1,0:T(1,128)S(1)}, f32[1,128]{1,0:T(1,128)S(1)}, u32[]{:S(2)}, u32[]{:S(2)}) collective-permute-start(f32[1,128]{1,0:T(1,128)S(1)} %bitcast.33), channel_id=1, source_target_pairs={{0,8},{8,0},{1,9},{9,1},{2,10},{10,2},{3,11},{11,3},{4,12},{12,4},... | collective-permute-start | bytes 1544 | tf_op jit(solution)/shard_map/ppermute | solution.py:160
  136.3 1.1 collective-permute-done.7
  137.5 1.0 multiply_convert_fusion.after_ref
  138.5 4.1 %reduce-scatter.2.cloned.1.call-done.grad_ref = bf16[2,288,256]{2,1,0:T(8,128)(2,1)} async-done(((bf16[2,2304,256]{2,1,0:T(8,128)(2,1)}), bf16[2,288,256]{2,1,0:T(8,128)(2,1)}) %reduce-scatter.2.cloned.1.call-update) | async-done | bytes 294928 | tf_op jit(solution)/shard_map/reduce_scatter | solution.py:217
  142.6 2.1 %gate_up_grads.1 = (bf16[2,288,256]{2,1,0:T(8,128)(2,1)}, bf16[2,288,256]{2,1,0:T(8,128)(2,1)}) custom-call(bf16[2,288,256]{2,1,0:T(8,128)(2,1)} %reduce-scatter.2.cloned.1.call-done.grad_ref, bf16[2,288,256]{2,1,0:T(8,128)(2,1)} %gate_ref.3, bf16[2,288,256]{2,1,0:T(8,128)(2,1)} %up_ref.3, bf16[2,256,768]{2,1,0:T(8,128)(2,1)} %multiply_convert_fusion.after_ref), custom_call_target="tpu_custom_call" | custom-call | tf_op jit(solution)/shard_map/gate_up_grads/pallas_call | solution.py:47
  (27 shorter events, 0.4 us)
Async XLA Ops:
  7.2 1.5 %copy-start = (bf16[128,768]{1,0:T(8,128)(2,1)S(1)}, bf16[128,768]{1,0:T(8,128)(2,1)}, u32[]{:S(2)}) copy-start(bf16[128,768]{1,0:T(8,128)(2,1)} %param.6) | copy-start | bytes 589828
  9.7 32.3 %all-to-all-start = ((bf16[8,72,768]{2,1,0:T(8,128)(2,1)}), bf16[8,72,768]{2,1,0:T(8,128)(2,1)S(1)}, u32[]{:S(2)}, u32[]{:S(2)}) async-start(bf16[8,72,768]{2,1,0:T(8,128)(2,1)} %broadcast_in_dim.6), calls=%async_computation | async-start | bytes 1769472 | tf_op jit(solution)/shard_map/all_to_all | solution.py:192
  16.8 79.6 %all-gather.2.cloned.1.call-start = ((), (), s32[]{:S(2)}) async-start(), calls=%async_computation.4 | async-start | bytes 2654208 | tf_op jit(solution)/shard_map/all_gather | solution.py:196
  18.8 123.9 %reduce-scatter.2.cloned.1.call-start = ((), (), s32[]{:S(2)}) async-start(), calls=%async_computation.5 | async-start | bytes 2654208 | tf_op jit(solution)/shard_map/reduce_scatter | solution.py:217
  42.1 23.6 %copy-start.1 = (bf16[8,72,768]{2,1,0:T(8,128)(2,1)}, bf16[8,72,768]{2,1,0:T(8,128)(2,1)S(1)}, u32[]{:S(2)}) copy-start(bf16[8,72,768]{2,1,0:T(8,128)(2,1)S(1)} %all-to-all-done.own_ref) | copy-start | bytes 2654212
  42.1 4.4 %collective-permute-start.2 = (bf16[8,72,768]{2,1,0:T(8,128)(2,1)S(1)}, bf16[8,72,768]{2,1,0:T(8,128)(2,1)}, u32[]{:S(2)}, u32[]{:S(2)}) collective-permute-start(bf16[8,72,768]{2,1,0:T(8,128)(2,1)S(1)} %all-to-all-done.own_ref), channel_id=1, source_target_pairs={{0,8},{8,0},{1,9},{9,1},{2,10},{10,2},{3,11},{11,3},{4,12},{12,4},... | collective-permute-start | bytes 2654216 | tf_op jit(solution)/shard_map/ppermute | solution.py:160
  44.0 14.9 %collective-permute-start = (bf16[8,72,768]{2,1,0:T(8,128)(2,1)S(1)}, bf16[8,72,768]{2,1,0:T(8,128)(2,1)S(1)}, u32[]{:S(2)}, u32[]{:S(2)}) collective-permute-start(bf16[8,72,768]{2,1,0:T(8,128)(2,1)S(1)} %all-to-all-done.own_ref), channel_id=1, source_target_pairs={{0,128},{8,392},{128,256},{136,8},{256,384},{264,136},{384,0},{392... | collective-permute-start | bytes 2654216 | tf_op jit(solution)/shard_map/ppermute | solution.py:169
  46.5 25.3 %collective-permute-start.3 = (bf16[8,72,768]{2,1,0:T(8,128)(2,1)}, bf16[8,72,768]{2,1,0:T(8,128)(2,1)}, u32[]{:S(2)}, u32[]{:S(2)}) collective-permute-start(bf16[8,72,768]{2,1,0:T(8,128)(2,1)} %collective-permute-done.2.other_ref), channel_id=1, source_target_pairs={{0,128},{8,392},{128,256},{136,8},{256,384},{264,136},{384,0},{392... | collective-permute-start | bytes 2654216 | tf_op jit(solution)/shard_map/ppermute | solution.py:169
  58.9 15.2 %copy-start.3 = (bf16[8,72,768]{2,1,0:T(8,128)(2,1)}, bf16[8,72,768]{2,1,0:T(8,128)(2,1)S(1)}, u32[]{:S(2)}) copy-start(bf16[8,72,768]{2,1,0:T(8,128)(2,1)S(1)} %collective-permute-done.own_ref) | copy-start | bytes 2654212
  58.9 21.3 %collective-permute-start.1 = (bf16[8,72,768]{2,1,0:T(8,128)(2,1)S(1)}, bf16[8,72,768]{2,1,0:T(8,128)(2,1)S(1)}, u32[]{:S(2)}, u32[]{:S(2)}) collective-permute-start(bf16[8,72,768]{2,1,0:T(8,128)(2,1)S(1)} %collective-permute-done.own_ref), channel_id=1, source_target_pairs={{0,128},{8,392},{128,256},{136,8},{256,384},{264,136},{384,0},{392... | collective-permute-start | bytes 2654216 | tf_op jit(solution)/shard_map/ppermute | solution.py:169
  63.7 19.6 %collective-permute-start.6 = (bf16[8,72,768]{2,1,0:T(8,128)(2,1)S(1)}, bf16[8,72,768]{2,1,0:T(8,128)(2,1)}, u32[]{:S(2)}, u32[]{:S(2)}) collective-permute-start(bf16[8,72,768]{2,1,0:T(8,128)(2,1)S(1)} %collective-permute-done.own_ref), channel_id=1, source_target_pairs={{0,8},{8,0},{1,9},{9,1},{2,10},{10,2},{3,11},{11,3},{4,12},{12,4},... | collective-permute-start | bytes 2654216 | tf_op jit(solution)/shard_map/ppermute | solution.py:160
  71.8 11.6 %collective-permute-start.5 = (bf16[8,72,768]{2,1,0:T(8,128)(2,1)}, bf16[8,72,768]{2,1,0:T(8,128)(2,1)S(1)}, u32[]{:S(2)}, u32[]{:S(2)}) collective-permute-start(bf16[8,72,768]{2,1,0:T(8,128)(2,1)} %collective-permute-done.3.other_ref), channel_id=1, source_target_pairs={{0,8},{8,0},{1,9},{9,1},{2,10},{10,2},{3,11},{11,3},{4,12},{12,4},... | collective-permute-start | bytes 2654216 | tf_op jit(solution)/shard_map/ppermute | solution.py:160
  80.2 10.1 %copy-start.2 = (bf16[8,72,768]{2,1,0:T(8,128)(2,1)}, bf16[8,72,768]{2,1,0:T(8,128)(2,1)S(1)}, u32[]{:S(2)}) copy-start(bf16[8,72,768]{2,1,0:T(8,128)(2,1)S(1)} %collective-permute-done.1.own_ref) | copy-start | bytes 2654212
  80.2 10.1 %collective-permute-start.4 = (bf16[8,72,768]{2,1,0:T(8,128)(2,1)S(1)}, bf16[8,72,768]{2,1,0:T(8,128)(2,1)}, u32[]{:S(2)}, u32[]{:S(2)}) collective-permute-start(bf16[8,72,768]{2,1,0:T(8,128)(2,1)S(1)} %collective-permute-done.1.own_ref), channel_id=1, source_target_pairs={{0,8},{8,0},{1,9},{9,1},{2,10},{10,2},{3,11},{11,3},{4,12},{12,4},... | collective-permute-start | bytes 2654216 | tf_op jit(solution)/shard_map/ppermute | solution.py:160
  83.3 0.9 copy-start.4
  134.4 3.0 %collective-permute-start.7 = (f32[1,128]{1,0:T(1,128)S(1)}, f32[1,128]{1,0:T(1,128)S(1)}, u32[]{:S(2)}, u32[]{:S(2)}) collective-permute-start(f32[1,128]{1,0:T(1,128)S(1)} %bitcast.33), channel_id=1, source_target_pairs={{0,8},{8,0},{1,9},{9,1},{2,10},{10,2},{3,11},{11,3},{4,12},{12,4},... | collective-permute-start | bytes 1544 | tf_op jit(solution)/shard_map/ppermute | solution.py:160
Sparse Core Ops, SparseCore 0:
  20.3 49.7 all-gather.1
  96.6 46.0 reduce-scatter.1

commit v3 on v2

v3 whole, which is shorter than its diff:
```python
import math

import jax
import jax.numpy as jnp
from jax import lax
from jax.experimental import pallas as pl
from jax.experimental.pallas import tpu as pltpu
from jax.sharding import Mesh
from jax.sharding import PartitionSpec as P

CAP = 72
META = 8
LANES = 128
X_CHIPS = 4
VMEM_GRANT = 16 * 2**20


def prepare_kernel(core_ref, rows_ref, ids_ref, probs_ref, gate_ref, up_ref, payload_ref, hidden_ref):
    lanes = payload_ref.shape[2]
    half = rows_ref.shape[0] // 2
    rows = rows_ref[pl.ds(core_ref[0] * half, half), :]
    probs = probs_ref[...]
    high = probs.astype(jnp.bfloat16).astype(jnp.float32)
    middle = (probs - high).astype(jnp.bfloat16).astype(jnp.float32)
    low = (probs - high) - middle
    lines = [ids_ref[...].astype(jnp.float32)]
    for route in range(probs.shape[0]):
        lines += [piece[route : route + 1] for piece in (high, middle, low)]
    meta = jnp.concatenate(lines, axis=0).astype(jnp.bfloat16)
    strips = [rows[:, start : start + lanes] for start in range(0, rows.shape[1], lanes)]
    payload = jnp.concatenate(strips + [meta], axis=0)
    for copy in range(payload_ref.shape[0]):
        payload_ref[copy] = payload
    gate = gate_ref[...].astype(jnp.float32)
    up = up_ref[...].astype(jnp.float32)
    hidden_ref[...] = (gate * jax.nn.sigmoid(gate) * up).astype(jnp.bfloat16)


def prepare(core, grad_rows, expert_ids, gate_probs, gate_pre, up_pre, copies):
    tokens, width = grad_rows.shape
    padded = tokens * width // (2 * LANES) + META
    operands = (grad_rows, expert_ids.T, gate_probs.T, gate_pre, up_pre)
    results = [
        jax.ShapeDtypeStruct((copies, padded, LANES), jnp.bfloat16),
        jax.ShapeDtypeStruct(gate_pre.shape, jnp.bfloat16),
    ]

    def whole(array):
        zeros = (0,) * len(array.shape)
        return pl.BlockSpec(array.shape, lambda i: zeros)

    return pl.pallas_call(
        prepare_kernel,
        grid=(1,),
        in_specs=[pl.BlockSpec(memory_space=pltpu.SMEM)] + [whole(operand) for operand in operands],
        out_specs=[whole(result) for result in results],
        out_shape=results,
        name="prepare",
    )(core.reshape(1), *operands)


def gate_up_kernel(grad_ref, gate_ref, up_ref, after_ref, gate_out_ref, up_out_ref):
    gate = gate_ref[0].astype(jnp.float32)
    up = up_ref[0].astype(jnp.float32)
    grad = grad_ref[0].astype(jnp.float32)
    sigmoid_gate = jax.nn.sigmoid(gate)
    gate_out_ref[0] = (grad * up * sigmoid_gate * (1.0 + gate * (1.0 - sigmoid_gate))).astype(jnp.bfloat16)
    up_out_ref[0] = (grad * (gate * sigmoid_gate)).astype(jnp.bfloat16)


def gate_up_grads(own_grad, gate_pre, up_pre, after):
    experts, rows, width = gate_pre.shape
    block = pl.BlockSpec((1, rows, width), lambda i: (i, 0, 0))
    return pl.pallas_call(
        gate_up_kernel,
        grid=(experts,),
        in_specs=[block, block, block, pl.BlockSpec(memory_space=pl.ANY)],
        out_specs=[block, block],
        out_shape=[jax.ShapeDtypeStruct(gate_pre.shape, jnp.bfloat16)] * 2,
        name="gate_up_grads",
    )(own_grad, gate_pre, up_pre, after)


def dispatch_kernel(place_ref, own_ref, other_ref, weight_ref, *refs):
    placed_ref, partial_ref = refs[-2:]
    step = pl.program_id(0)
    meta_start = own_ref.shape[1] - META
    experts_here, width, _ = weight_ref.shape
    half = meta_start * LANES // width
    tokens = 2 * half
    blocks = placed_ref.shape[1] // CAP
    before = lax.broadcasted_iota(jnp.int32, (tokens, tokens), 0)
    after = lax.broadcasted_iota(jnp.int32, (tokens, tokens), 1)
    earlier = (before < after).astype(jnp.bfloat16)
    slot_row = lax.broadcasted_iota(jnp.int32, (CAP, tokens), 0).astype(jnp.float32)
    core = place_ref[4]
    first = (core * experts_here).astype(jnp.float32)
    members, probs = [], []
    for block in range(blocks):
        meta = own_ref[step * blocks + block, meta_start : meta_start + META, :].astype(jnp.float32)
        first_id, second_id = meta[0:1], meta[1:2]
        first_prob = (meta[2:3] + meta[3:4]) + meta[4:5]
        second_prob = (meta[5:6] + meta[6:7]) + meta[7:8]
        for expert in range(experts_here):
            one = first_id == first + expert
            two = second_id == first + expert
            members.append(jnp.logical_or(one, two).astype(jnp.float32))
            probs.append(jnp.where(one, first_prob, jnp.where(two, second_prob, 0.0)))
    member = jnp.concatenate(members, axis=0)
    slots = jnp.dot(member.astype(jnp.bfloat16), earlier, preferred_element_type=jnp.float32)
    slots = jnp.where(member > 0.0, slots, -1.0)
    prob = jnp.concatenate(probs, axis=0)
    slots = jnp.where(core == 1, pltpu.roll(slots, half, 1), slots)
    prob = jnp.where(core == 1, pltpu.roll(prob, half, 1), prob)
    for block in range(blocks):
        index = step * blocks + block
        strips = [
            jnp.concatenate([ref[index, start : start + half, :] for ref in (own_ref, other_ref)], axis=0)
            for start in range(0, meta_start, half)
        ]
        tokens_here = jnp.concatenate(strips, axis=1)
        chosen, scales = [], []
        for expert in range(experts_here):
            line = block * experts_here + expert
            match = (slot_row == slots[line : line + 1]).astype(jnp.float32)
            chosen.append(match)
            scales.append(jnp.sum(match * prob[line : line + 1], axis=1, keepdims=True))
        picked = jnp.dot(
            jnp.concatenate(chosen, axis=0).astype(jnp.bfloat16),
            tokens_here,
            preferred_element_type=jnp.float32,
        )
        scaled = (picked * jnp.concatenate(scales, axis=0)).astype(jnp.bfloat16)
        for expert in range(experts_here):
            placed_ref[expert, block * CAP : (block + 1) * CAP, :] = scaled[expert * CAP : (expert + 1) * CAP]
    for expert in range(experts_here):
        partial_ref[expert] = jnp.dot(
            placed_ref[expert], weight_ref[expert], preferred_element_type=jnp.float32
        ).astype(jnp.bfloat16)


def dispatch_and_project(turn, places, own_half, other_half, weight, rows, owners, buffers):
    experts_here, width, hidden_width = weight.shape
    steps = 2
    per_owner = rows // owners
    resident = pl.BlockSpec(memory_space=pltpu.VMEM)
    anywhere = [pl.BlockSpec(memory_space=pltpu.HBM)] * len(buffers)
    return pl.pallas_call(
        dispatch_kernel,
        grid_spec=pltpu.PrefetchScalarGridSpec(
            num_scalar_prefetch=1,
            grid=(steps,),
            in_specs=[resident, resident, resident] + anywhere,
            out_specs=[
                pl.BlockSpec((experts_here, per_owner, width), lambda i, s: (0, s[turn] * steps + i, 0)),
                pl.BlockSpec((experts_here, per_owner, hidden_width), lambda i, s: (0, s[turn] * steps + i, 0)),
            ],
        ),
        out_shape=[
            pltpu.HBM((experts_here, rows, width), jnp.bfloat16),
            pltpu.HBM((experts_here, rows, hidden_width), jnp.bfloat16),
        ],
        input_output_aliases={4 + i: i for i in range(len(buffers))},
        compiler_params=pltpu.CompilerParams(dimension_semantics=("arbitrary",), vmem_limit_bytes=VMEM_GRANT),
        name="dispatch_project",
    )(places, own_half, other_half, weight, *buffers)


def weight_grad_kernel(hidden_ref, placed_ref, grad_ref, squares_ref, total_ref):
    expert = pl.program_id(0)
    grad = lax.dot_general(
        hidden_ref[0], placed_ref[0], (((0,), (0,)), ((), ())), preferred_element_type=jnp.float32
    )
    grad_ref[0] = grad
    squares = jnp.sum(grad * grad, axis=0, keepdims=True)

    @pl.when(expert == 0)
    def _():
        total_ref[...] = squares

    @pl.when(expert > 0)
    def _():
        total_ref[...] += squares

    @pl.when(expert == pl.num_programs(0) - 1)
    def _():
        squares_ref[...] = jnp.full(squares_ref.shape, jnp.sum(total_ref[...]), jnp.float32)


def weight_grads(hidden_all, arrived, copies):
    experts, rows, hidden_width = hidden_all.shape
    width = arrived.shape[2]
    return pl.pallas_call(
        weight_grad_kernel,
        grid=(experts,),
        in_specs=[
            pl.BlockSpec((1, rows, hidden_width), lambda i: (i, 0, 0)),
            pl.BlockSpec((1, rows, width), lambda i: (i, 0, 0)),
        ],
        out_specs=[
            pl.BlockSpec((1, hidden_width, width), lambda i: (i, 0, 0)),
            pl.BlockSpec((copies, 1, LANES), lambda i: (0, 0, 0)),
        ],
        out_shape=[
            jax.ShapeDtypeStruct((experts, hidden_width, width), jnp.float32),
            jax.ShapeDtypeStruct((copies, 1, LANES), jnp.float32),
        ],
        scratch_shapes=[pltpu.VMEM((1, width), jnp.float32)],
        compiler_params=pltpu.CompilerParams(dimension_semantics=("arbitrary",)),
        name="weight_grads",
    )(hidden_all, arrived)


def exchange(value, axis):
    return lax.all_to_all(value, axis, 0, 0, tiled=True)


def to_all(value, axis):
    return exchange(jnp.broadcast_to(value[None], (lax.axis_size(axis),) + value.shape), axis)


def swap_cores(value):
    return lax.ppermute(value, "expert", [(0, 1), (1, 0)])


def along_x(value):
    size = lax.axis_size("x")
    pairs = []
    for place in range(size):
        pairs.append((place * 2, (place + 1) % size * 2))
        pairs.append((place * 2 + 1, (place - 1) % size * 2 + 1))
    return lax.ppermute(value, ("x", "expert"), pairs)


def on_device(grad_rows, gate_probs, expert_ids, gate_pre, up_pre, down_weight):
    experts_here, rows_here, hidden_width = gate_pre.shape
    tokens_here, feature_width = grad_rows.shape
    cores = lax.axis_size("expert")
    planes = lax.axis_size("x")
    lines = lax.axis_size("y")
    sources = planes * lines
    owners = lax.axis_size("ffn")
    experts_total = experts_here * cores
    core = lax.axis_index("expert")
    plane = lax.axis_index("x")
    rows = rows_here * owners

    payload, hidden = prepare(core, grad_rows, expert_ids, gate_probs, gate_pre, up_pre, lines)
    near = exchange(payload, "y")
    hidden_all = lax.all_gather(hidden, "ffn", axis=1, tiled=True)
    weight = jnp.swapaxes(down_weight, 1, 2)
    offsets = [0, planes - 1 + 2 * core, 1 + planes - 2 * core, 2]
    places = jnp.stack([(plane + offset) % planes for offset in offsets] + [core]).astype(jnp.int32)

    def project(turn, own_half, other_half, buffers):
        return dispatch_and_project(
            turn, places, own_half, other_half, weight, rows, owners, buffers
        )

    side_own = along_x(near)
    near_other = swap_cores(near)
    side_other = along_x(near_other)
    buffers = project(0, near, near_other, ())
    side_own, buffers = lax.optimization_barrier((side_own, buffers))
    far_own = along_x(side_own)
    beyond_other = swap_cores(side_own)
    beyond_own = swap_cores(side_other)
    buffers = project(1, side_own, side_other, buffers)
    far_own, buffers = lax.optimization_barrier((far_own, buffers))
    far_other = swap_cores(far_own)
    buffers = project(2, beyond_own, beyond_other, buffers)
    arrived, partial_terms = project(3, far_own, far_other, buffers)
    own_grad = lax.psum_scatter(partial_terms, "ffn", scatter_dimension=1, tiled=True)

    weight_grad, squares = weight_grads(hidden_all, arrived, sources)
    squares = jnp.sum(exchange(squares, ("x", "y")), axis=0)
    squares = jnp.sum(to_all(squares, ("expert", "ffn"))[:, 0, 0])
    entry_count = (
        float(experts_total) * float(hidden_width * sources) * float(feature_width * owners)
    )
    clip_limit = jnp.float32(0.5 * math.sqrt(entry_count))
    factor = clip_limit / jnp.maximum(jnp.sqrt(squares), clip_limit)
    down_grad = (weight_grad * factor).astype(jnp.bfloat16)

    gate_grad, up_grad = gate_up_grads(own_grad, gate_pre, up_pre, down_grad)
    return (down_grad, gate_grad, up_grad)


def solution(mesh):
    fine = Mesh(mesh.devices.reshape((X_CHIPS, -1) + mesh.devices.shape[1:]), ("x", "y", "expert", "ffn"))
    spread = ("x", "y")
    placed = (
        P(spread, "ffn"),
        P(spread, None),
        P(spread, None),
        P("expert", "ffn", spread),
        P("expert", "ffn", spread),
        P("expert", spread, "ffn"),
    )
    return jax.shard_map(
        on_device,
        mesh=fine,
        in_specs=placed,
        out_specs=(P("expert", spread, "ffn"), P("expert", "ffn", spread), P("expert", "ffn", spread)),
        check_vma=False,
    )
```

time: 152 us -> 138 us (0.908)
  blocking collectives: 30.7 us -> 61 us
  waiting for transfers between devices: 37.7 us -> 15.1 us
  starting transfers between devices: 26.6 us -> 18.2 us
  matrix products: 6.55 us -> 0 us
  Pallas kernels: 28.2 us -> 23.5 us
  other arithmetic: 4.86 us -> 3.08 us
    all_to_all x2 -> x3, blocking collectives: 30.7 us -> 61 us  [exchange(): return lax.all_to_all(value, axis, 0, 0, tiled=True)]
    all_to_all x1 -> x0, waiting for transfers between devices: 23.2 us -> none  [on_device(): lax.all_to_all(jnp.broadcast_to(payload[None], (lines,) + payload.shape),...]
    pallas_call x4, Pallas kernels: 24.3 us -> 13.1 us  [dispatch_and_project(): pl.pallas_call(dispatch_kernel, grid_spec=pltpu.PrefetchScalarGridSpec(nu...]
    all_to_all x1 -> x0, starting transfers between devices: 7.1 us -> none  [on_device(): lax.all_to_all(jnp.broadcast_to(payload[None], (lines,) + payload.shape),...]
    dot_general x1 -> x0, matrix products: 6.55 us -> none  [on_device(): jnp.einsum('erf,erd->efd', hidden_all, arrived, preferred_element_type=jn...]
    pallas_call x1 -> x2, Pallas kernels: 1.87 us -> 8.28 us  [the longest x1 6.02 us: weight_grads(): pl.pallas_call(weight_grad_kernel, grid=(experts,), in_specs=[pl.BlockSpe...]
    another operation x5 -> x0, other arithmetic: 3.06 us -> none  [the longest x4 2.3 us: dispatch_and_project(): jnp.stack([plane, core]).astype(jnp.int32)]
    reduce_scatter x1, waiting for transfers between devices: 4.12 us -> 5.75 us  [on_device(): lax.psum_scatter(partial_terms, 'ffn', scatter_dimension=1, tiled=True)]
  transfers between devices with their start and end apart: 11 -> 9, of which waited for: 5 -> 4; matrix products, arithmetic and copies ran while one was open for 7% -> 3% of each run, Pallas kernels for 17% -> 14%
where the time goes in v3:
time: 138 us; the launch traced here: 137 us
  blocking collectives  61 us (44%)
  Pallas kernels  23.5 us (17%)
  starting transfers between devices  18.2 us (13%)
  waiting for transfers between devices  15.1 us (11%)
  between operations  14.9 us (11%)
  other arithmetic  3.08 us (2%)
  local copies, waits for them, and re-layouts  1.51 us (1%)
    all_to_all x3, blocking collectives, exchange(): return lax.all_to_all(value, axis, 0, 0, tiled=True)  61 us
    pallas_call x4, Pallas kernels, dispatch_and_project(): pl.pallas_call(dispatch_kernel, grid_spec=pltpu.PrefetchScalarGridSpec(nu...  13.1 us
    ppermute x3, starting transfers between devices, along_x(): return lax.ppermute(value, ('x', 'expert'), pairs)  9.35 us
    ppermute x3, waiting for transfers between devices, along_x(): return lax.ppermute(value, ('x', 'expert'), pairs)  9.32 us
    ppermute x4, starting transfers between devices, swap_cores(): return lax.ppermute(value, 'expert', [(0, 1), (1, 0)])  8.74 us
    pallas_call x1, Pallas kernels, weight_grads(): pl.pallas_call(weight_grad_kernel, grid=(experts,), in_specs=[pl.BlockSpe...  6.02 us
    reduce_scatter x1, waiting for transfers between devices, on_device(): lax.psum_scatter(partial_terms, 'ffn', scatter_dimension=1, tiled=True)  5.75 us
  transfers between devices with their start and end apart: 9, of which 4 were waited for; matrix products, arithmetic and copies ran while one was open for 3% of the time, Pallas kernels for 14%

profile of v3, /device:TPU:6, one launch (start us, length us, event | category | flops | bytes accessed | tf_op | source)
XLA Modules:
  0.0 137.3 jit_solution(7350726167903815947)
XLA Ops:
  7.2 0.0 all-gather.2.cloned.1.call-start
  7.2 2.3 %prepare.1 = (bf16[8,392,128]{2,1,0:T(8,128)(2,1)}, bf16[2,288,256]{2,1,0:T(8,128)(2,1)}) custom-call(s32[1]{0:T(128)} %bitcast.core_ref, bf16[128,768]{1,0:T(8,128)(2,1)} %rows_ref.1, s32[2,128]{1,0:T(2,128)} %bitcast.12, f32[2,128]{1,0:T(2,128)} %bitcast.13, bf16[2,288,256]{2,1,0:T(8,128)(2,1)} %gate_ref.3, bf16[2,288,256]{2,1,0:T(8,128)(2,1)} %up_ref.3), custom_call_target="tpu_custom_call" | custom-call | tf_op jit(solution)/shard_map/prepare/pallas_call | solution.py:52
  9.5 0.0 all-gather.2.cloned.1.call-update
  9.5 0.0 reduce-scatter.2.cloned.1.call-start
  9.6 30.6 %all_to_all.15.own_ref = bf16[8,392,128]{2,1,0:T(8,128)(2,1)S(1)} all-to-all(bf16[8,392,128]{2,1,0:T(8,128)(2,1)} %get-tuple-element.24), channel_id=1, replica_groups=mesh['x'=4,'y'=8,'expert'=2,'ffn'=8] {'y'}, dimensions={0} | all-to-all | bytes 1605632 | tf_op jit(solution)/shard_map/all_to_all | solution.py:215
  40.1 1.9 %collective-permute-start.1 = (bf16[8,392,128]{2,1,0:T(8,128)(2,1)S(1)}, bf16[8,392,128]{2,1,0:T(8,128)(2,1)S(1)}, u32[]{:S(2)}, u32[]{:S(2)}) collective-permute-start(bf16[8,392,128]{2,1,0:T(8,128)(2,1)S(1)} %all_to_all.15.own_ref), channel_id=1, source_target_pairs={{0,8},{8,0},{1,9},{9,1},{2,10},{10,2},{3,11},{11,3},{4,12},{12,4},... | collective-permute-start | bytes 2408456 | tf_op jit(solution)/shard_map/ppermute | solution.py:223
  42.0 2.4 %collective-permute-start = (bf16[8,392,128]{2,1,0:T(8,128)(2,1)S(1)}, bf16[8,392,128]{2,1,0:T(8,128)(2,1)S(1)}, u32[]{:S(2)}, u32[]{:S(2)}) collective-permute-start(bf16[8,392,128]{2,1,0:T(8,128)(2,1)S(1)} %all_to_all.15.own_ref), channel_id=1, source_target_pairs={{0,128},{8,392},{128,256},{136,8},{256,384},{264,136},{384,0},{392... | collective-permute-start | bytes 2408456 | tf_op jit(solution)/shard_map/ppermute | solution.py:232
  44.5 1.4 %copy.17 = bf16[2,256,768]{1,2,0:T(8,128)(2,1)S(1)} copy(bf16[2,256,768]{2,1,0:T(8,128)(2,1)} %param.11) | data formatting | bytes 1572864 | tf_op args[5]
  45.9 0.1 stack.20.place_ref
  46.0 0.0 collective-permute-done.1.other_ref
  46.0 3.4 %collective-permute-start.3 = (bf16[8,392,128]{2,1,0:T(8,128)(2,1)S(1)}, bf16[8,392,128]{2,1,0:T(8,128)(2,1)S(1)}, u32[]{:S(2)}, u32[]{:S(2)}) collective-permute-start(bf16[8,392,128]{2,1,0:T(8,128)(2,1)S(1)} %collective-permute-done.1.other_ref), channel_id=1, source_target_pairs={{0,128},{8,392},{128,256},{136,8},{256,384},{264,136},{384,0},{392... | collective-permute-start | bytes 2408456 | tf_op jit(solution)/shard_map/ppermute | solution.py:232
  49.4 3.3 %dispatch_project.4 = (bf16[2,2304,768]{2,1,0:T(8,128)(2,1)}, bf16[2,2304,256]{2,1,0:T(8,128)(2,1)}) custom-call(s32[5]{0:T(128)S(1)} %stack.20.place_ref, bf16[8,392,128]{2,1,0:T(8,128)(2,1)S(1)} %all_to_all.15.own_ref, bf16[8,392,128]{2,1,0:T(8,128)(2,1)S(1)} %collective-permute-done.1.other_ref, bf16[2,768,256]{2,1,0:T(8,128)(2,1)S(1)} %bitcast.8), custom_call_target="tpu_custom_call" | custom-call | tf_op jit(solution)/shard_map/dispatch_project/pallas_call | solution.py:148
  52.7 3.4 %collective-permute-done.own_ref = bf16[8,392,128]{2,1,0:T(8,128)(2,1)S(1)} collective-permute-done((bf16[8,392,128]{2,1,0:T(8,128)(2,1)S(1)}, bf16[8,392,128]{2,1,0:T(8,128)(2,1)S(1)}, u32[]{:S(2)}, u32[]{:S(2)}) %collective-permute-start) | collective-permute-done | bytes 802848 | tf_op jit(solution)/shard_map/ppermute | solution.py:232
  56.1 3.6 %collective-permute-start.2 = (bf16[8,392,128]{2,1,0:T(8,128)(2,1)S(1)}, bf16[8,392,128]{2,1,0:T(8,128)(2,1)S(1)}, u32[]{:S(2)}, u32[]{:S(2)}) collective-permute-start(bf16[8,392,128]{2,1,0:T(8,128)(2,1)S(1)} %collective-permute-done.own_ref), channel_id=1, source_target_pairs={{0,128},{8,392},{128,256},{136,8},{256,384},{264,136},{384,0},{392... | collective-permute-start | bytes 2408456 | tf_op jit(solution)/shard_map/ppermute | solution.py:232
  59.7 1.9 %collective-permute-start.6 = (bf16[8,392,128]{2,1,0:T(8,128)(2,1)S(1)}, bf16[8,392,128]{2,1,0:T(8,128)(2,1)S(1)}, u32[]{:S(2)}, u32[]{:S(2)}) collective-permute-start(bf16[8,392,128]{2,1,0:T(8,128)(2,1)S(1)} %collective-permute-done.own_ref), channel_id=1, source_target_pairs={{0,8},{8,0},{1,9},{9,1},{2,10},{10,2},{3,11},{11,3},{4,12},{12,4},... | collective-permute-start | bytes 2408456 | tf_op jit(solution)/shard_map/ppermute | solution.py:223
  61.6 3.1 %collective-permute-done.3.other_ref = bf16[8,392,128]{2,1,0:T(8,128)(2,1)S(1)} collective-permute-done((bf16[8,392,128]{2,1,0:T(8,128)(2,1)S(1)}, bf16[8,392,128]{2,1,0:T(8,128)(2,1)S(1)}, u32[]{:S(2)}, u32[]{:S(2)}) %collective-permute-start.3) | collective-permute-done | bytes 802848 | tf_op jit(solution)/shard_map/ppermute | solution.py:232
  64.7 2.5 %collective-permute-start.5 = (bf16[8,392,128]{2,1,0:T(8,128)(2,1)S(1)}, bf16[8,392,128]{2,1,0:T(8,128)(2,1)S(1)}, u32[]{:S(2)}, u32[]{:S(2)}) collective-permute-start(bf16[8,392,128]{2,1,0:T(8,128)(2,1)S(1)} %collective-permute-done.3.other_ref), channel_id=1, source_target_pairs={{0,8},{8,0},{1,9},{9,1},{2,10},{10,2},{3,11},{11,3},{4,12},{12,4},... | collective-permute-start | bytes 2408456 | tf_op jit(solution)/shard_map/ppermute | solution.py:223
  67.2 3.3 %dispatch_project.5 = (bf16[2,2304,768]{2,1,0:T(8,128)(2,1)}, bf16[2,2304,256]{2,1,0:T(8,128)(2,1)}) custom-call(s32[5]{0:T(128)S(1)} %stack.20.place_ref, bf16[8,392,128]{2,1,0:T(8,128)(2,1)S(1)} %collective-permute-done.own_ref, bf16[8,392,128]{2,1,0:T(8,128)(2,1)S(1)} %collective-permute-done.3.other_ref, ...), custom_call_target="tpu_custom_call", output_to_operand_aliasing={{0}: (4, {}), {1}: (5, {})} | custom-call | tf_op jit(solution)/shard_map/dispatch_project/pallas_call | solution.py:148
  70.5 2.8 %collective-permute-done.2.own_ref = bf16[8,392,128]{2,1,0:T(8,128)(2,1)S(1)} collective-permute-done((bf16[8,392,128]{2,1,0:T(8,128)(2,1)S(1)}, bf16[8,392,128]{2,1,0:T(8,128)(2,1)S(1)}, u32[]{:S(2)}, u32[]{:S(2)}) %collective-permute-start.2) | collective-permute-done | bytes 802848 | tf_op jit(solution)/shard_map/ppermute | solution.py:232
  73.3 2.5 %collective-permute-start.4 = (bf16[8,392,128]{2,1,0:T(8,128)(2,1)S(1)}, bf16[8,392,128]{2,1,0:T(8,128)(2,1)S(1)}, u32[]{:S(2)}, u32[]{:S(2)}) collective-permute-start(bf16[8,392,128]{2,1,0:T(8,128)(2,1)S(1)} %collective-permute-done.2.own_ref), channel_id=1, source_target_pairs={{0,8},{8,0},{1,9},{9,1},{2,10},{10,2},{3,11},{11,3},{4,12},{12,4},... | collective-permute-start | bytes 2408456 | tf_op jit(solution)/shard_map/ppermute | solution.py:223
  75.8 3.3 %dispatch_project.6 = (bf16[2,2304,768]{2,1,0:T(8,128)(2,1)}, bf16[2,2304,256]{2,1,0:T(8,128)(2,1)}) custom-call(s32[5]{0:T(128)S(1)} %stack.20.place_ref, bf16[8,392,128]{2,1,0:T(8,128)(2,1)S(1)} %collective-permute-done.5.own_ref, bf16[8,392,128]{2,1,0:T(8,128)(2,1)S(1)} %collective-permute-done.6.other_ref, ...), custom_call_target="tpu_custom_call", output_to_operand_aliasing={{0}: (4, {}), {1}: (5, {})} | custom-call | tf_op jit(solution)/shard_map/dispatch_project/pallas_call | solution.py:148
  79.1 3.3 %dispatch_project.7 = (bf16[2,2304,768]{2,1,0:T(8,128)(2,1)}, bf16[2,2304,256]{2,1,0:T(8,128)(2,1)}) custom-call(s32[5]{0:T(128)S(1)} %stack.20.place_ref, bf16[8,392,128]{2,1,0:T(8,128)(2,1)S(1)} %collective-permute-done.2.own_ref, bf16[8,392,128]{2,1,0:T(8,128)(2,1)S(1)} %collective-permute-done.4.other_ref, ...), custom_call_target="tpu_custom_call", output_to_operand_aliasing={{0}: (4, {}), {1}: (5, {})} | custom-call | tf_op jit(solution)/shard_map/dispatch_project/pallas_call | solution.py:148
  82.3 0.0 reduce-scatter.2.cloned.1.call-update
  82.4 0.0 all-gather.2.cloned.1.call-done.hidden_ref
  82.4 6.0 %weight_grads.1 = (f32[2,256,768]{2,1,0:T(8,128)}, f32[32,1,128]{2,1,0:T(1,128)}) custom-call(bf16[2,2304,256]{2,1,0:T(8,128)(2,1)} %all-gather.2.cloned.1.call-done.hidden_ref, bf16[2,2304,768]{2,1,0:T(8,128)(2,1)} %get-tuple-element.37.placed_ref), custom_call_target="tpu_custom_call" | custom-call | tf_op jit(solution)/shard_map/weight_grads/pallas_call | solution.py:193
  88.4 12.6 %all_to_all.16 = f32[32,1,128]{2,1,0:T(1,128)S(1)} all-to-all(f32[32,1,128]{2,1,0:T(1,128)} %get-tuple-element.39), channel_id=1, replica_groups=mesh['x'=4,'y'=8,'expert'=2,'ffn'=8] {'x','y'}, dimensions={0} | all-to-all | bytes 32768 | tf_op jit(solution)/shard_map/all_to_all | solution.py:215
  101.0 0.1 reduce_sum.18
  101.1 17.8 %all_to_all.17 = f32[16,1,128]{2,1,0:T(1,128)S(1)} all-to-all(f32[16,1,128]{2,1,0:T(1,128)S(1)} %broadcast_in_dim.2), channel_id=1, replica_groups=mesh['x'=4,'y'=8,'expert'=2,'ffn'=8] {'expert','ffn'}, dimensions={0} | all-to-all | bytes 16384 | tf_op jit(solution)/shard_map/all_to_all | solution.py:215
  118.9 0.6 slice_reduce_fusion
  120.2 2.4 %multiply_convert_fusion.after_ref = bf16[2,256,768]{2,1,0:T(8,128)(2,1)} fusion(f32[2,256,768]{2,1,0:T(8,128)} %get-tuple-element.38, f32[]{:T(128)S(6)} %div.3), kind=kLoop, calls=%fused_computation | loop fusion | flops 786432 | bytes 2359300 | tf_op jit(solution)/shard_map/convert_element_type | solution.py:283
  122.7 5.7 %reduce-scatter.2.cloned.1.call-done.grad_ref = bf16[2,288,256]{2,1,0:T(8,128)(2,1)} async-done(((bf16[2,2304,256]{2,1,0:T(8,128)(2,1)}), bf16[2,288,256]{2,1,0:T(8,128)(2,1)}) %reduce-scatter.2.cloned.1.call-update) | async-done | bytes 294928 | tf_op jit(solution)/shard_map/reduce_scatter | solution.py:273
  128.4 2.1 %gate_up_grads.1 = (bf16[2,288,256]{2,1,0:T(8,128)(2,1)}, bf16[2,288,256]{2,1,0:T(8,128)(2,1)}) custom-call(bf16[2,288,256]{2,1,0:T(8,128)(2,1)} %reduce-scatter.2.cloned.1.call-done.grad_ref, bf16[2,288,256]{2,1,0:T(8,128)(2,1)} %gate_ref.3, bf16[2,288,256]{2,1,0:T(8,128)(2,1)} %up_ref.3, bf16[2,256,768]{2,1,0:T(8,128)(2,1)} %multiply_convert_fusion.after_ref), custom_call_target="tpu_custom_call" | custom-call | tf_op jit(solution)/shard_map/gate_up_grads/pallas_call | solution.py:74
  (4 shorter events, 0.0 us)
Async XLA Ops:
  7.2 75.2 %all-gather.2.cloned.1.call-start = ((), (), s32[]{:S(2)}) async-start(), calls=%async_computation.4 | async-start | bytes 2654208 | tf_op jit(solution)/shard_map/all_gather | solution.py:250
  9.5 118.9 %reduce-scatter.2.cloned.1.call-start = ((), (), s32[]{:S(2)}) async-start(), calls=%async_computation.5 | async-start | bytes 2654208 | tf_op jit(solution)/shard_map/reduce_scatter | solution.py:273
  40.1 5.9 %collective-permute-start.1 = (bf16[8,392,128]{2,1,0:T(8,128)(2,1)S(1)}, bf16[8,392,128]{2,1,0:T(8,128)(2,1)S(1)}, u32[]{:S(2)}, u32[]{:S(2)}) collective-permute-start(bf16[8,392,128]{2,1,0:T(8,128)(2,1)S(1)} %all_to_all.15.own_ref), channel_id=1, source_target_pairs={{0,8},{8,0},{1,9},{9,1},{2,10},{10,2},{3,11},{11,3},{4,12},{12,4},... | collective-permute-start | bytes 2408456 | tf_op jit(solution)/shard_map/ppermute | solution.py:223
  42.0 14.1 %collective-permute-start = (bf16[8,392,128]{2,1,0:T(8,128)(2,1)S(1)}, bf16[8,392,128]{2,1,0:T(8,128)(2,1)S(1)}, u32[]{:S(2)}, u32[]{:S(2)}) collective-permute-start(bf16[8,392,128]{2,1,0:T(8,128)(2,1)S(1)} %all_to_all.15.own_ref), channel_id=1, source_target_pairs={{0,128},{8,392},{128,256},{136,8},{256,384},{264,136},{384,0},{392... | collective-permute-start | bytes 2408456 | tf_op jit(solution)/shard_map/ppermute | solution.py:232
  46.0 18.7 %collective-permute-start.3 = (bf16[8,392,128]{2,1,0:T(8,128)(2,1)S(1)}, bf16[8,392,128]{2,1,0:T(8,128)(2,1)S(1)}, u32[]{:S(2)}, u32[]{:S(2)}) collective-permute-start(bf16[8,392,128]{2,1,0:T(8,128)(2,1)S(1)} %collective-permute-done.1.other_ref), channel_id=1, source_target_pairs={{0,128},{8,392},{128,256},{136,8},{256,384},{264,136},{384,0},{392... | collective-permute-start | bytes 2408456 | tf_op jit(solution)/shard_map/ppermute | solution.py:232
  56.1 17.2 %collective-permute-start.2 = (bf16[8,392,128]{2,1,0:T(8,128)(2,1)S(1)}, bf16[8,392,128]{2,1,0:T(8,128)(2,1)S(1)}, u32[]{:S(2)}, u32[]{:S(2)}) collective-permute-start(bf16[8,392,128]{2,1,0:T(8,128)(2,1)S(1)} %collective-permute-done.own_ref), channel_id=1, source_target_pairs={{0,128},{8,392},{128,256},{136,8},{256,384},{264,136},{384,0},{392... | collective-permute-start | bytes 2408456 | tf_op jit(solution)/shard_map/ppermute | solution.py:232
  59.7 16.1 %collective-permute-start.6 = (bf16[8,392,128]{2,1,0:T(8,128)(2,1)S(1)}, bf16[8,392,128]{2,1,0:T(8,128)(2,1)S(1)}, u32[]{:S(2)}, u32[]{:S(2)}) collective-permute-start(bf16[8,392,128]{2,1,0:T(8,128)(2,1)S(1)} %collective-permute-done.own_ref), channel_id=1, source_target_pairs={{0,8},{8,0},{1,9},{9,1},{2,10},{10,2},{3,11},{11,3},{4,12},{12,4},... | collective-permute-start | bytes 2408456 | tf_op jit(solution)/shard_map/ppermute | solution.py:223
  64.7 11.1 %collective-permute-start.5 = (bf16[8,392,128]{2,1,0:T(8,128)(2,1)S(1)}, bf16[8,392,128]{2,1,0:T(8,128)(2,1)S(1)}, u32[]{:S(2)}, u32[]{:S(2)}) collective-permute-start(bf16[8,392,128]{2,1,0:T(8,128)(2,1)S(1)} %collective-permute-done.3.other_ref), channel_id=1, source_target_pairs={{0,8},{8,0},{1,9},{9,1},{2,10},{10,2},{3,11},{11,3},{4,12},{12,4},... | collective-permute-start | bytes 2408456 | tf_op jit(solution)/shard_map/ppermute | solution.py:223
  73.3 5.7 %collective-permute-start.4 = (bf16[8,392,128]{2,1,0:T(8,128)(2,1)S(1)}, bf16[8,392,128]{2,1,0:T(8,128)(2,1)S(1)}, u32[]{:S(2)}, u32[]{:S(2)}) collective-permute-start(bf16[8,392,128]{2,1,0:T(8,128)(2,1)S(1)} %collective-permute-done.2.own_ref), channel_id=1, source_target_pairs={{0,8},{8,0},{1,9},{9,1},{2,10},{10,2},{3,11},{11,3},{4,12},{12,4},... | collective-permute-start | bytes 2408456 | tf_op jit(solution)/shard_map/ppermute | solution.py:223
Sparse Core Ops, SparseCore 0:
  10.7 49.6 all-gather.1
  82.5 45.8 reduce-scatter.1

commit v4 on v3

--- a/solution.py
+++ b/solution.py
@@ -1,3 +1,4 @@
+import functools
 import math
 
 import jax
@@ -76,28 +77,31 @@
         grid=(experts,),
         in_specs=[block, block, block, pl.BlockSpec(memory_space=pl.ANY)],
         out_specs=[block, block],
-        out_shape=[jax.ShapeDtypeStruct(gate_pre.shape, jnp.bfloat16)] * 2,
+        out_shape=[pltpu.HBM(gate_pre.shape, jnp.bfloat16)] * 2,
+        compiler_params=pltpu.CompilerParams(vmem_limit_bytes=VMEM_GRANT),
         name="gate_up_grads",
-    )(own_grad, gate_pre, up_pre, after)
-
-
-def dispatch_kernel(place_ref, own_ref, other_ref, weight_ref, *refs):
-    placed_ref, partial_ref = refs[-2:]
-    step = pl.program_id(0)
+    )(pltpu.with_memory_space_constraint(own_grad, pltpu.HBM), gate_pre, up_pre, after)
+
+
+def dispatch_kernel(turn, place_ref, own_ref, other_ref, weight_ref, *refs):
+    placed_out, partial_out, placed_ref, partial_ref, placed_sems, partial_sems = refs[-6:]
+    sources = own_ref.shape[0]
     meta_start = own_ref.shape[1] - META
     experts_here, width, _ = weight_ref.shape
     half = meta_start * LANES // width
     tokens = 2 * half
-    blocks = placed_ref.shape[1] // CAP
+    steps = partial_ref.shape[0]
+    blocks = sources // steps
     before = lax.broadcasted_iota(jnp.int32, (tokens, tokens), 0)
     after = lax.broadcasted_iota(jnp.int32, (tokens, tokens), 1)
     earlier = (before < after).astype(jnp.bfloat16)
     slot_row = lax.broadcasted_iota(jnp.int32, (CAP, tokens), 0).astype(jnp.float32)
+    plane = place_ref[turn]
     core = place_ref[4]
     first = (core * experts_here).astype(jnp.float32)
     members, probs = [], []
-    for block in range(blocks):
-        meta = own_ref[step * blocks + block, meta_start : meta_start + META, :].astype(jnp.float32)
+    for block in range(sources):
+        meta = own_ref[block, meta_start : meta_start + META, :].astype(jnp.float32)
         first_id, second_id = meta[0:1], meta[1:2]
         first_prob = (meta[2:3] + meta[3:4]) + meta[4:5]
         second_prob = (meta[5:6] + meta[6:7]) + meta[7:8]
@@ -112,10 +116,10 @@
     prob = jnp.concatenate(probs, axis=0)
     slots = jnp.where(core == 1, pltpu.roll(slots, half, 1), slots)
     prob = jnp.where(core == 1, pltpu.roll(prob, half, 1), prob)
-    for block in range(blocks):
-        index = step * blocks + block
+    copies = []
+    for block in range(sources):
         strips = [
-            jnp.concatenate([ref[index, start : start + half, :] for ref in (own_ref, other_ref)], axis=0)
+            jnp.concatenate([ref[block, start : start + half, :] for ref in (own_ref, other_ref)], axis=0)
             for start in range(0, meta_start, half)
         ]
         tokens_here = jnp.concatenate(strips, axis=1)
@@ -133,35 +137,62 @@
         scaled = (picked * jnp.concatenate(scales, axis=0)).astype(jnp.bfloat16)
         for expert in range(experts_here):
             placed_ref[expert, block * CAP : (block + 1) * CAP, :] = scaled[expert * CAP : (expert + 1) * CAP]
-    for expert in range(experts_here):
-        partial_ref[expert] = jnp.dot(
-            placed_ref[expert], weight_ref[expert], preferred_element_type=jnp.float32
-        ).astype(jnp.bfloat16)
+        if block % 2 == 1:
+            start = (block - 1) * CAP
+            target = pl.multiple_of(plane * (sources * CAP) + start, 2 * CAP)
+            for expert in range(experts_here):
+                copies.append(
+                    pltpu.make_async_copy(
+                        placed_ref.at[expert, pl.ds(start, 2 * CAP), :],
+                        placed_out.at[expert, pl.ds(target, 2 * CAP), :],
+                        placed_sems.at[block // 2, expert],
+                    )
+                )
+                copies[-1].start()
+        if block % blocks == blocks - 1:
+            step = block // blocks
+            for expert in range(experts_here):
+                partial_ref[step, expert] = jnp.dot(
+                    placed_ref[expert, step * blocks * CAP : (step + 1) * blocks * CAP, :],
+                    weight_ref[expert],
+                    preferred_element_type=jnp.float32,
+                ).astype(jnp.bfloat16)
+                copies.append(
+                    pltpu.make_async_copy(
+                        partial_ref.at[step, expert],
+                        partial_out.at[plane * steps + step, expert],
+                        partial_sems.at[step, expert],
+                    )
+                )
+                copies[-1].start()
+    for copy in copies:
+        copy.wait()
 
 
 def dispatch_and_project(turn, places, own_half, other_half, weight, rows, owners, buffers):
     experts_here, width, hidden_width = weight.shape
+    sources = own_half.shape[0]
     steps = 2
     per_owner = rows // owners
     resident = pl.BlockSpec(memory_space=pltpu.VMEM)
-    anywhere = [pl.BlockSpec(memory_space=pltpu.HBM)] * len(buffers)
+    outside = pl.BlockSpec(memory_space=pltpu.HBM)
     return pl.pallas_call(
-        dispatch_kernel,
-        grid_spec=pltpu.PrefetchScalarGridSpec(
-            num_scalar_prefetch=1,
-            grid=(steps,),
-            in_specs=[resident, resident, resident] + anywhere,
-            out_specs=[
-                pl.BlockSpec((experts_here, per_owner, width), lambda i, s: (0, s[turn] * steps + i, 0)),
-                pl.BlockSpec((experts_here, per_owner, hidden_width), lambda i, s: (0, s[turn] * steps + i, 0)),
-            ],
-        ),
+        functools.partial(dispatch_kernel, turn),
+        in_specs=[pl.BlockSpec(memory_space=pltpu.SMEM), resident, resident, resident]
+        + [outside] * len(buffers),
+        out_specs=[outside, outside],
         out_shape=[
             pltpu.HBM((experts_here, rows, width), jnp.bfloat16),
-            pltpu.HBM((experts_here, rows, hidden_width), jnp.bfloat16),
+            pltpu.HBM((owners, experts_here, per_owner, hidden_width), jnp.bfloat16),
+        ],
+        scratch_shapes=[
+            pltpu.VMEM((experts_here, steps * per_owner, width), jnp.bfloat16),
+            pltpu.VMEM((steps, experts_here, per_owner, hidden_width), jnp.bfloat16),
+            pltpu.SemaphoreType.DMA((sources // 2, experts_here)),
+            pltpu.SemaphoreType.DMA((steps, experts_here)),
         ],
         input_output_aliases={4 + i: i for i in range(len(buffers))},
-        compiler_params=pltpu.CompilerParams(dimension_semantics=("arbitrary",), vmem_limit_bytes=VMEM_GRANT),
+        compiler_params=pltpu.CompilerParams(vmem_limit_bytes=VMEM_GRANT),
         name="dispatch_project",
     )(places, own_half, other_half, weight, *buffers)
 
@@ -206,9 +237,14 @@
             jax.ShapeDtypeStruct((copies, 1, LANES), jnp.float32),
         ],
         scratch_shapes=[pltpu.VMEM((1, width), jnp.float32)],
-        compiler_params=pltpu.CompilerParams(dimension_semantics=("arbitrary",)),
+        compiler_params=pltpu.CompilerParams(
+            dimension_semantics=("arbitrary",), vmem_limit_bytes=2 * VMEM_GRANT
+        ),
         name="weight_grads",
-    )(hidden_all, arrived)
+    )(
+        pltpu.with_memory_space_constraint(hidden_all, pltpu.HBM),
+        pltpu.with_memory_space_constraint(arrived, pltpu.HBM),
+    )
 
 
 def exchange(value, axis):
@@ -270,7 +306,7 @@
     far_other = swap_cores(far_own)
     buffers = project(2, beyond_own, beyond_other, buffers)
     arrived, partial_terms = project(3, far_own, far_other, buffers)
-    own_grad = lax.psum_scatter(partial_terms, "ffn", scatter_dimension=1, tiled=True)
+    own_grad = lax.psum_scatter(partial_terms, "ffn", scatter_dimension=0, tiled=True)[0]
 
     weight_grad, squares = weight_grads(hidden_all, arrived, sources)
     squares = jnp.sum(exchange(squares, ("x", "y")), axis=0)

time: 138 us -> 136 us (0.986)
  waiting for transfers between devices: 15.1 us -> 19.5 us
  Pallas kernels: 23.5 us -> 20 us
  other arithmetic: 3.08 us -> 0.78 us
    reduce_scatter x1, waiting for transfers between devices: 5.75 us -> 8.84 us  [on_device(): lax.psum_scatter(partial_terms, 'ffn', scatter_dimension=0, tiled=True)[0]]
    pallas_call x4, Pallas kernels: 13.1 us -> 10.7 us  [dispatch_and_project(): pl.pallas_call(functools.partial(dispatch_kernel, turn), in_specs=[pl.Blo...]
    convert_element_type x1, other arithmetic: 2.41 us -> 0.11 us  [on_device(): down_grad = (weight_grad * factor).astype(jnp.bfloat16)]
  transfers between devices with their start and end apart: 9 -> 9, of which waited for: 4 -> 4; matrix products, arithmetic and copies ran while one was open for 3% -> 2% of each run, Pallas kernels for 14% -> 12%
where the time goes in v4:
time: 136 us
  blocking collectives  60.9 us (45%)
  Pallas kernels  20 us (15%)
  waiting for transfers between devices  19.5 us (14%)
  starting transfers between devices  18.2 us (13%)
  between operations  15 us (11%)
  local copies, waits for them, and re-layouts  1.53 us (1%)
    all_to_all x3, blocking collectives, exchange(): return lax.all_to_all(value, axis, 0, 0, tiled=True)  60.9 us
    pallas_call x4, Pallas kernels, dispatch_and_project(): pl.pallas_call(functools.partial(dispatch_kernel, turn), in_specs=[pl.Blo...  10.7 us
    ppermute x3, waiting for transfers between devices, along_x(): return lax.ppermute(value, ('x', 'expert'), pairs)  10.5 us
    ppermute x3, starting transfers between devices, along_x(): return lax.ppermute(value, ('x', 'expert'), pairs)  9.35 us
    reduce_scatter x1, waiting for transfers between devices, on_device(): lax.psum_scatter(partial_terms, 'ffn', scatter_dimension=0, tiled=True)[0]  8.84 us
    ppermute x4, starting transfers between devices, swap_cores(): return lax.ppermute(value, 'expert', [(0, 1), (1, 0)])  8.74 us
    pallas_call x1, Pallas kernels, weight_grads(): pl.pallas_call(weight_grad_kernel, grid=(experts,), in_specs=[pl.BlockSpe...  5.1 us
  transfers between devices with their start and end apart: 9, of which 4 were waited for; matrix products, arithmetic and copies ran while one was open for 2% of the time, Pallas kernels for 12%

profile of v4, /device:TPU:6, one launch (start us, length us, event | category | flops | bytes accessed | tf_op | source)
XLA Modules:
  0.0 135.9 jit_solution(1605936706457752660)
XLA Ops:
  7.2 0.0 all-gather.2.cloned.1.call-start
  7.2 2.3 %prepare.1 = (bf16[8,392,128]{2,1,0:T(8,128)(2,1)}, bf16[2,288,256]{2,1,0:T(8,128)(2,1)}) custom-call(s32[1]{0:T(128)} %bitcast.core_ref, bf16[128,768]{1,0:T(8,128)(2,1)} %rows_ref.1, s32[2,128]{1,0:T(2,128)} %bitcast.14, f32[2,128]{1,0:T(2,128)} %bitcast.15, bf16[2,288,256]{2,1,0:T(8,128)(2,1)} %gate_ref.3, bf16[2,288,256]{2,1,0:T(8,128)(2,1)} %up_ref.3), custom_call_target="tpu_custom_call" | custom-call | tf_op jit(solution)/shard_map/prepare/pallas_call | solution.py:53
  9.5 0.0 all-gather.2.cloned.1.call-update
  9.5 0.0 reduce-scatter.2.cloned.1.call-start
  9.6 30.6 %all_to_all.15.own_ref = bf16[8,392,128]{2,1,0:T(8,128)(2,1)S(1)} all-to-all(bf16[8,392,128]{2,1,0:T(8,128)(2,1)} %get-tuple-element.24), channel_id=1, replica_groups=mesh['x'=4,'y'=8,'expert'=2,'ffn'=8] {'y'}, dimensions={0} | all-to-all | bytes 1605632 | tf_op jit(solution)/shard_map/all_to_all | solution.py:251
  40.1 1.9 %collective-permute-start.1 = (bf16[8,392,128]{2,1,0:T(8,128)(2,1)S(1)}, bf16[8,392,128]{2,1,0:T(8,128)(2,1)S(1)}, u32[]{:S(2)}, u32[]{:S(2)}) collective-permute-start(bf16[8,392,128]{2,1,0:T(8,128)(2,1)S(1)} %all_to_all.15.own_ref), channel_id=1, source_target_pairs={{0,8},{8,0},{1,9},{9,1},{2,10},{10,2},{3,11},{11,3},{4,12},{12,4},... | collective-permute-start | bytes 2408456 | tf_op jit(solution)/shard_map/ppermute | solution.py:259
  42.0 2.4 %collective-permute-start = (bf16[8,392,128]{2,1,0:T(8,128)(2,1)S(1)}, bf16[8,392,128]{2,1,0:T(8,128)(2,1)S(1)}, u32[]{:S(2)}, u32[]{:S(2)}) collective-permute-start(bf16[8,392,128]{2,1,0:T(8,128)(2,1)S(1)} %all_to_all.15.own_ref), channel_id=1, source_target_pairs={{0,128},{8,392},{128,256},{136,8},{256,384},{264,136},{384,0},{392... | collective-permute-start | bytes 2408456 | tf_op jit(solution)/shard_map/ppermute | solution.py:268
  44.5 1.4 %copy.17 = bf16[2,256,768]{1,2,0:T(8,128)(2,1)S(1)} copy(bf16[2,256,768]{2,1,0:T(8,128)(2,1)} %param.11) | data formatting | bytes 1572864 | tf_op args[5]
  45.9 0.1 stack.20.place_ref
  46.0 3.4 %collective-permute-start.3 = (bf16[8,392,128]{2,1,0:T(8,128)(2,1)S(1)}, bf16[8,392,128]{2,1,0:T(8,128)(2,1)S(1)}, u32[]{:S(2)}, u32[]{:S(2)}) collective-permute-start(bf16[8,392,128]{2,1,0:T(8,128)(2,1)S(1)} %collective-permute-done.1.other_ref), channel_id=1, source_target_pairs={{0,128},{8,392},{128,256},{136,8},{256,384},{264,136},{384,0},{392... | collective-permute-start | bytes 2408456 | tf_op jit(solution)/shard_map/ppermute | solution.py:268
  49.4 2.7 %dispatch_project.4 = (bf16[2,2304,768]{2,1,0:T(8,128)(2,1)}, bf16[8,2,288,256]{3,2,1,0:T(8,128)(2,1)}) custom-call(s32[5]{0:T(128)S(1)} %stack.20.place_ref, bf16[8,392,128]{2,1,0:T(8,128)(2,1)S(1)} %all_to_all.15.own_ref, bf16[8,392,128]{2,1,0:T(8,128)(2,1)S(1)} %collective-permute-done.1.other_ref, bf16[2,768,256]{2,1,0:T(8,128)(2,1)S(1)} %bitcast.9), custom_call_target="tpu_custom_call" | custom-call | tf_op jit(solution)/shard_map/dispatch_project/pallas_call | solution.py:179
  52.1 4.0 %collective-permute-done.own_ref = bf16[8,392,128]{2,1,0:T(8,128)(2,1)S(1)} collective-permute-done((bf16[8,392,128]{2,1,0:T(8,128)(2,1)S(1)}, bf16[8,392,128]{2,1,0:T(8,128)(2,1)S(1)}, u32[]{:S(2)}, u32[]{:S(2)}) %collective-permute-start) | collective-permute-done | bytes 802848 | tf_op jit(solution)/shard_map/ppermute | solution.py:268
  56.1 3.6 %collective-permute-start.2 = (bf16[8,392,128]{2,1,0:T(8,128)(2,1)S(1)}, bf16[8,392,128]{2,1,0:T(8,128)(2,1)S(1)}, u32[]{:S(2)}, u32[]{:S(2)}) collective-permute-start(bf16[8,392,128]{2,1,0:T(8,128)(2,1)S(1)} %collective-permute-done.own_ref), channel_id=1, source_target_pairs={{0,128},{8,392},{128,256},{136,8},{256,384},{264,136},{384,0},{392... | collective-permute-start | bytes 2408456 | tf_op jit(solution)/shard_map/ppermute | solution.py:268
  59.7 1.9 %collective-permute-start.6 = (bf16[8,392,128]{2,1,0:T(8,128)(2,1)S(1)}, bf16[8,392,128]{2,1,0:T(8,128)(2,1)S(1)}, u32[]{:S(2)}, u32[]{:S(2)}) collective-permute-start(bf16[8,392,128]{2,1,0:T(8,128)(2,1)S(1)} %collective-permute-done.own_ref), channel_id=1, source_target_pairs={{0,8},{8,0},{1,9},{9,1},{2,10},{10,2},{3,11},{11,3},{4,12},{12,4},... | collective-permute-start | bytes 2408456 | tf_op jit(solution)/shard_map/ppermute | solution.py:259
  61.6 3.1 %collective-permute-done.3.other_ref = bf16[8,392,128]{2,1,0:T(8,128)(2,1)S(1)} collective-permute-done((bf16[8,392,128]{2,1,0:T(8,128)(2,1)S(1)}, bf16[8,392,128]{2,1,0:T(8,128)(2,1)S(1)}, u32[]{:S(2)}, u32[]{:S(2)}) %collective-permute-start.3) | collective-permute-done | bytes 802848 | tf_op jit(solution)/shard_map/ppermute | solution.py:268
  64.7 2.5 %collective-permute-start.5 = (bf16[8,392,128]{2,1,0:T(8,128)(2,1)S(1)}, bf16[8,392,128]{2,1,0:T(8,128)(2,1)S(1)}, u32[]{:S(2)}, u32[]{:S(2)}) collective-permute-start(bf16[8,392,128]{2,1,0:T(8,128)(2,1)S(1)} %collective-permute-done.3.other_ref), channel_id=1, source_target_pairs={{0,8},{8,0},{1,9},{9,1},{2,10},{10,2},{3,11},{11,3},{4,12},{12,4},... | collective-permute-start | bytes 2408456 | tf_op jit(solution)/shard_map/ppermute | solution.py:259
  67.2 2.7 %dispatch_project.5 = (bf16[2,2304,768]{2,1,0:T(8,128)(2,1)}, bf16[8,2,288,256]{3,2,1,0:T(8,128)(2,1)}) custom-call(s32[5]{0:T(128)S(1)} %stack.20.place_ref, bf16[8,392,128]{2,1,0:T(8,128)(2,1)S(1)} %collective-permute-done.own_ref, bf16[8,392,128]{2,1,0:T(8,128)(2,1)S(1)} %collective-permute-done.3.other_ref, ...), custom_call_target="tpu_custom_call", output_to_operand_aliasing={{0}: (4, {}), {1}: (5, {})} | custom-call | tf_op jit(solution)/shard_map/dispatch_project/pallas_call | solution.py:179
  69.8 3.5 %collective-permute-done.2.own_ref = bf16[8,392,128]{2,1,0:T(8,128)(2,1)S(1)} collective-permute-done((bf16[8,392,128]{2,1,0:T(8,128)(2,1)S(1)}, bf16[8,392,128]{2,1,0:T(8,128)(2,1)S(1)}, u32[]{:S(2)}, u32[]{:S(2)}) %collective-permute-start.2) | collective-permute-done | bytes 802848 | tf_op jit(solution)/shard_map/ppermute | solution.py:268
  73.3 2.5 %collective-permute-start.4 = (bf16[8,392,128]{2,1,0:T(8,128)(2,1)S(1)}, bf16[8,392,128]{2,1,0:T(8,128)(2,1)S(1)}, u32[]{:S(2)}, u32[]{:S(2)}) collective-permute-start(bf16[8,392,128]{2,1,0:T(8,128)(2,1)S(1)} %collective-permute-done.2.own_ref), channel_id=1, source_target_pairs={{0,8},{8,0},{1,9},{9,1},{2,10},{10,2},{3,11},{11,3},{4,12},{12,4},... | collective-permute-start | bytes 2408456 | tf_op jit(solution)/shard_map/ppermute | solution.py:259
  75.8 2.7 %dispatch_project.6 = (bf16[2,2304,768]{2,1,0:T(8,128)(2,1)}, bf16[8,2,288,256]{3,2,1,0:T(8,128)(2,1)}) custom-call(s32[5]{0:T(128)S(1)} %stack.20.place_ref, bf16[8,392,128]{2,1,0:T(8,128)(2,1)S(1)} %collective-permute-done.5.own_ref, bf16[8,392,128]{2,1,0:T(8,128)(2,1)S(1)} %collective-permute-done.6.other_ref, ...), custom_call_target="tpu_custom_call", output_to_operand_aliasing={{0}: (4, {}), {1}: (5, {})} | custom-call | tf_op jit(solution)/shard_map/dispatch_project/pallas_call | solution.py:179
  78.5 2.7 %dispatch_project.7 = (bf16[2,2304,768]{2,1,0:T(8,128)(2,1)}, bf16[8,2,288,256]{3,2,1,0:T(8,128)(2,1)}) custom-call(s32[5]{0:T(128)S(1)} %stack.20.place_ref, bf16[8,392,128]{2,1,0:T(8,128)(2,1)S(1)} %collective-permute-done.2.own_ref, bf16[8,392,128]{2,1,0:T(8,128)(2,1)S(1)} %collective-permute-done.4.other_ref, ...), custom_call_target="tpu_custom_call", output_to_operand_aliasing={{0}: (4, {}), {1}: (5, {})} | custom-call | tf_op jit(solution)/shard_map/dispatch_project/pallas_call | solution.py:179
  81.2 0.0 reduce-scatter.2.cloned.1.call-update
  81.2 0.0 all-gather.2.cloned.1.call-done.hidden_ref
  81.3 5.1 %weight_grads.1 = (f32[2,256,768]{2,1,0:T(8,128)S(1)}, f32[32,1,128]{2,1,0:T(1,128)S(1)}) custom-call(bf16[2,2304,256]{2,1,0:T(8,128)(2,1)} %all-gather.2.cloned.1.call-done.hidden_ref, bf16[2,2304,768]{2,1,0:T(8,128)(2,1)} %get-tuple-element.37.placed_ref), custom_call_target="tpu_custom_call" | custom-call | tf_op jit(solution)/shard_map/weight_grads/pallas_call | solution.py:224
  86.4 12.6 %all_to_all.16 = f32[32,1,128]{2,1,0:T(1,128)S(1)} all-to-all(f32[32,1,128]{2,1,0:T(1,128)S(1)} %get-tuple-element.39), channel_id=1, replica_groups=mesh['x'=4,'y'=8,'expert'=2,'ffn'=8] {'x','y'}, dimensions={0} | all-to-all | bytes 32768 | tf_op jit(solution)/shard_map/all_to_all | solution.py:251
  98.9 0.1 reduce_sum.18
  99.0 17.8 %all_to_all.17 = f32[16,1,128]{2,1,0:T(1,128)S(1)} all-to-all(f32[16,1,128]{2,1,0:T(1,128)S(1)} %broadcast_in_dim.2), channel_id=1, replica_groups=mesh['x'=4,'y'=8,'expert'=2,'ffn'=8] {'expert','ffn'}, dimensions={0} | all-to-all | bytes 16384 | tf_op jit(solution)/shard_map/all_to_all | solution.py:251
  116.8 0.6 slice_reduce_fusion
  118.2 0.1 multiply_convert_fusion.after_ref
  118.3 0.0 copy-start
  118.3 8.8 %reduce-scatter.2.cloned.1.call-done = bf16[1,2,288,256]{3,2,1,0:T(8,128)(2,1)} async-done(((bf16[8,2,288,256]{3,2,1,0:T(8,128)(2,1)}), bf16[1,2,288,256]{3,2,1,0:T(8,128)(2,1)}) %reduce-scatter.2.cloned.1.call-update) | async-done | bytes 294928 | tf_op jit(solution)/shard_map/reduce_scatter | solution.py:309
  127.2 1.9 %gate_up_grads.1 = (bf16[2,288,256]{2,1,0:T(8,128)(2,1)}, bf16[2,288,256]{2,1,0:T(8,128)(2,1)}) custom-call(bf16[2,288,256]{2,1,0:T(8,128)(2,1)} %bitcast.13, bf16[2,288,256]{2,1,0:T(8,128)(2,1)S(1)} %copy-done.1, bf16[2,288,256]{2,1,0:T(8,128)(2,1)S(1)} %copy-done.2, bf16[2,256,768]{2,1,0:T(8,128)(2,1)S(1)} %multiply_convert_fusion.after_ref), custom_call_target="tpu_custom_call" | custom-call | tf_op jit(solution)/shard_map/gate_up_grads/pallas_call | solution.py:75
  (10 shorter events, 0.0 us)
Async XLA Ops:
  7.2 74.1 %all-gather.2.cloned.1.call-start = ((), (), s32[]{:S(2)}) async-start(), calls=%async_computation.4 | async-start | bytes 2654208 | tf_op jit(solution)/shard_map/all_gather | solution.py:286
  9.5 117.6 %reduce-scatter.2.cloned.1.call-start = ((), (), s32[]{:S(2)}) async-start(), calls=%async_computation.5 | async-start | bytes 2654208 | tf_op jit(solution)/shard_map/reduce_scatter | solution.py:309
  40.1 5.9 %collective-permute-start.1 = (bf16[8,392,128]{2,1,0:T(8,128)(2,1)S(1)}, bf16[8,392,128]{2,1,0:T(8,128)(2,1)S(1)}, u32[]{:S(2)}, u32[]{:S(2)}) collective-permute-start(bf16[8,392,128]{2,1,0:T(8,128)(2,1)S(1)} %all_to_all.15.own_ref), channel_id=1, source_target_pairs={{0,8},{8,0},{1,9},{9,1},{2,10},{10,2},{3,11},{11,3},{4,12},{12,4},... | collective-permute-start | bytes 2408456 | tf_op jit(solution)/shard_map/ppermute | solution.py:259
  42.0 14.1 %collective-permute-start = (bf16[8,392,128]{2,1,0:T(8,128)(2,1)S(1)}, bf16[8,392,128]{2,1,0:T(8,128)(2,1)S(1)}, u32[]{:S(2)}, u32[]{:S(2)}) collective-permute-start(bf16[8,392,128]{2,1,0:T(8,128)(2,1)S(1)} %all_to_all.15.own_ref), channel_id=1, source_target_pairs={{0,128},{8,392},{128,256},{136,8},{256,384},{264,136},{384,0},{392... | collective-permute-start | bytes 2408456 | tf_op jit(solution)/shard_map/ppermute | solution.py:268
  46.0 18.7 %collective-permute-start.3 = (bf16[8,392,128]{2,1,0:T(8,128)(2,1)S(1)}, bf16[8,392,128]{2,1,0:T(8,128)(2,1)S(1)}, u32[]{:S(2)}, u32[]{:S(2)}) collective-permute-start(bf16[8,392,128]{2,1,0:T(8,128)(2,1)S(1)} %collective-permute-done.1.other_ref), channel_id=1, source_target_pairs={{0,128},{8,392},{128,256},{136,8},{256,384},{264,136},{384,0},{392... | collective-permute-start | bytes 2408456 | tf_op jit(solution)/shard_map/ppermute | solution.py:268
  56.1 17.2 %collective-permute-start.2 = (bf16[8,392,128]{2,1,0:T(8,128)(2,1)S(1)}, bf16[8,392,128]{2,1,0:T(8,128)(2,1)S(1)}, u32[]{:S(2)}, u32[]{:S(2)}) collective-permute-start(bf16[8,392,128]{2,1,0:T(8,128)(2,1)S(1)} %collective-permute-done.own_ref), channel_id=1, source_target_pairs={{0,128},{8,392},{128,256},{136,8},{256,384},{264,136},{384,0},{392... | collective-permute-start | bytes 2408456 | tf_op jit(solution)/shard_map/ppermute | solution.py:268
  59.7 16.1 %collective-permute-start.6 = (bf16[8,392,128]{2,1,0:T(8,128)(2,1)S(1)}, bf16[8,392,128]{2,1,0:T(8,128)(2,1)S(1)}, u32[]{:S(2)}, u32[]{:S(2)}) collective-permute-start(bf16[8,392,128]{2,1,0:T(8,128)(2,1)S(1)} %collective-permute-done.own_ref), channel_id=1, source_target_pairs={{0,8},{8,0},{1,9},{9,1},{2,10},{10,2},{3,11},{11,3},{4,12},{12,4},... | collective-permute-start | bytes 2408456 | tf_op jit(solution)/shard_map/ppermute | solution.py:259
  64.7 11.1 %collective-permute-start.5 = (bf16[8,392,128]{2,1,0:T(8,128)(2,1)S(1)}, bf16[8,392,128]{2,1,0:T(8,128)(2,1)S(1)}, u32[]{:S(2)}, u32[]{:S(2)}) collective-permute-start(bf16[8,392,128]{2,1,0:T(8,128)(2,1)S(1)} %collective-permute-done.3.other_ref), channel_id=1, source_target_pairs={{0,8},{8,0},{1,9},{9,1},{2,10},{10,2},{3,11},{11,3},{4,12},{12,4},... | collective-permute-start | bytes 2408456 | tf_op jit(solution)/shard_map/ppermute | solution.py:259
  73.3 5.2 %collective-permute-start.4 = (bf16[8,392,128]{2,1,0:T(8,128)(2,1)S(1)}, bf16[8,392,128]{2,1,0:T(8,128)(2,1)S(1)}, u32[]{:S(2)}, u32[]{:S(2)}) collective-permute-start(bf16[8,392,128]{2,1,0:T(8,128)(2,1)S(1)} %collective-permute-done.2.own_ref), channel_id=1, source_target_pairs={{0,8},{8,0},{1,9},{9,1},{2,10},{10,2},{3,11},{11,3},{4,12},{12,4},... | collective-permute-start | bytes 2408456 | tf_op jit(solution)/shard_map/ppermute | solution.py:259
  86.4 40.8 %copy-start.1 = (bf16[2,288,256]{2,1,0:T(8,128)(2,1)S(1)}, bf16[2,288,256]{2,1,0:T(8,128)(2,1)}, u32[]{:S(2)}) copy-start(bf16[2,288,256]{2,1,0:T(8,128)(2,1)} %gate_ref.3) | copy-start | bytes 884740
  86.4 40.8 %copy-start.2 = (bf16[2,288,256]{2,1,0:T(8,128)(2,1)S(1)}, bf16[2,288,256]{2,1,0:T(8,128)(2,1)}, u32[]{:S(2)}) copy-start(bf16[2,288,256]{2,1,0:T(8,128)(2,1)} %up_ref.3) | copy-start | bytes 884740
  118.3 10.8 %copy-start = (bf16[2,256,768]{2,1,0:T(8,128)(2,1)}, bf16[2,256,768]{2,1,0:T(8,128)(2,1)S(1)}, u32[]{:S(2)}) copy-start(bf16[2,256,768]{2,1,0:T(8,128)(2,1)S(1)} %multiply_convert_fusion.after_ref) | copy-start | bytes 2359300
Sparse Core Ops, SparseCore 0:
  10.7 49.6 all-gather.1
  81.3 45.7 reduce-scatter.1

commit v5 on v4

--- a/solution.py
+++ b/solution.py
@@ -40,44 +40,72 @@
 def prepare(core, grad_rows, expert_ids, gate_probs, gate_pre, up_pre, copies):
     tokens, width = grad_rows.shape
     padded = tokens * width // (2 * LANES) + META
-    operands = (grad_rows, expert_ids.T, gate_probs.T, gate_pre, up_pre)
-    results = [
-        jax.ShapeDtypeStruct((copies, padded, LANES), jnp.bfloat16),
-        jax.ShapeDtypeStruct(gate_pre.shape, jnp.bfloat16),
-    ]
-
-    def whole(array):
-        zeros = (0,) * len(array.shape)
-        return pl.BlockSpec(array.shape, lambda i: zeros)
-
+    experts, rows_here, hidden_width = gate_pre.shape
+    small = (grad_rows, expert_ids.T, gate_probs.T)
+    block = pl.BlockSpec((1, rows_here, hidden_width), lambda i: (i, 0, 0))
     return pl.pallas_call(
         prepare_kernel,
-        grid=(1,),
-        in_specs=[pl.BlockSpec(memory_space=pltpu.SMEM)] + [whole(operand) for operand in operands],
-        out_specs=[whole(result) for result in results],
-        out_shape=results,
+        grid=(experts,),
+        in_specs=[pl.BlockSpec(memory_space=pltpu.SMEM)]
+        + [pl.BlockSpec(array.shape, lambda i: (0, 0)) for array in small]
+        + [block, block],
+        out_specs=[pl.BlockSpec((copies // experts, padded, LANES), lambda i: (i, 0, 0)), block],
+        out_shape=[
+            jax.ShapeDtypeStruct((copies, padded, LANES), jnp.bfloat16),
+            jax.ShapeDtypeStruct(gate_pre.shape, jnp.bfloat16),
+        ],
         name="prepare",
-    )(core.reshape(1), *operands)
-
-
-def gate_up_kernel(grad_ref, gate_ref, up_ref, after_ref, gate_out_ref, up_out_ref):
-    gate = gate_ref[0].astype(jnp.float32)
-    up = up_ref[0].astype(jnp.float32)
-    grad = grad_ref[0].astype(jnp.float32)
-    sigmoid_gate = jax.nn.sigmoid(gate)
-    gate_out_ref[0] = (grad * up * sigmoid_gate * (1.0 + gate * (1.0 - sigmoid_gate))).astype(jnp.bfloat16)
-    up_out_ref[0] = (grad * (gate * sigmoid_gate)).astype(jnp.bfloat16)
+    )(core.reshape(1), *small, gate_pre, up_pre)
+
+
+def gate_up_kernel(grad_in, gate_ref, up_ref, after_ref, gate_out, up_out,
+                   grad_ref, gate_out_ref, up_out_ref, load_sems, store_sems):
+    experts, rows, _ = gate_ref.shape
+    parts = load_sems.shape[1]
+    size = rows // parts
+    spots = [(expert, part) for expert in range(experts) for part in range(parts)]
+    loads = []
+    for expert, part in spots:
+        spot = (expert, pl.ds(part * size, size))
+        loads.append(pltpu.make_async_copy(grad_in.at[spot], grad_ref.at[spot], load_sems.at[expert, part]))
+        loads[-1].start()
+    stores = []
+    for load, (expert, part) in zip(loads, spots):
+        load.wait()
+        spot = (expert, pl.ds(part * size, size))
+        gate = gate_ref[spot].astype(jnp.float32)
+        up = up_ref[spot].astype(jnp.float32)
+        grad = grad_ref[spot].astype(jnp.float32)
+        sigmoid_gate = jax.nn.sigmoid(gate)
+        slope = sigmoid_gate * (1.0 + gate * (1.0 - sigmoid_gate))
+        gate_out_ref[spot] = (grad * up * slope).astype(jnp.bfloat16)
+        up_out_ref[spot] = (grad * (gate * sigmoid_gate)).astype(jnp.bfloat16)
+        for index, (source, target) in enumerate(((gate_out_ref, gate_out), (up_out_ref, up_out))):
+            stores.append(
+                pltpu.make_async_copy(source.at[spot], target.at[spot], store_sems.at[index, expert, part])
+            )
+            stores[-1].start()
+    for store in stores:
+        store.wait()
 
 
 def gate_up_grads(own_grad, gate_pre, up_pre, after):
-    experts, rows, width = gate_pre.shape
-    block = pl.BlockSpec((1, rows, width), lambda i: (i, 0, 0))
+    parts = 2
+    resident = pl.BlockSpec(memory_space=pltpu.VMEM)
+    outside = pl.BlockSpec(memory_space=pltpu.HBM)
+    shaped = pltpu.VMEM(gate_pre.shape, jnp.bfloat16)
     return pl.pallas_call(
         gate_up_kernel,
-        grid=(experts,),
-        in_specs=[block, block, block, pl.BlockSpec(memory_space=pl.ANY)],
-        out_specs=[block, block],
+        in_specs=[outside, resident, resident, pl.BlockSpec(memory_space=pl.ANY)],
+        out_specs=[outside, outside],
         out_shape=[pltpu.HBM(gate_pre.shape, jnp.bfloat16)] * 2,
+        scratch_shapes=[
+            shaped,
+            shaped,
+            shaped,
+            pltpu.SemaphoreType.DMA((gate_pre.shape[0], parts)),
+            pltpu.SemaphoreType.DMA((2, gate_pre.shape[0], parts)),
+        ],
         compiler_params=pltpu.CompilerParams(vmem_limit_bytes=VMEM_GRANT),
         name="gate_up_grads",
     )(pltpu.with_memory_space_constraint(own_grad, pltpu.HBM), gate_pre, up_pre, after)

time: 136 us -> 136 us (level)
  no operation moved by 1% of the time
where the time goes in v5:
time: 136 us
  blocking collectives  60.9 us (45%)
  Pallas kernels  19.9 us (15%)
  waiting for transfers between devices  19.4 us (14%)
  starting transfers between devices  18.2 us (13%)
  between operations  15 us (11%)
  local copies, waits for them, and re-layouts  1.53 us (1%)
    all_to_all x3, blocking collectives, exchange(): return lax.all_to_all(value, axis, 0, 0, tiled=True)  60.9 us
    pallas_call x4, Pallas kernels, dispatch_and_project(): pl.pallas_call(functools.partial(dispatch_kernel, turn), in_specs=[pl.Blo...  10.7 us
    ppermute x3, waiting for transfers between devices, along_x(): return lax.ppermute(value, ('x', 'expert'), pairs)  10.5 us
    ppermute x3, starting transfers between devices, along_x(): return lax.ppermute(value, ('x', 'expert'), pairs)  9.36 us
    reduce_scatter x1, waiting for transfers between devices, on_device(): lax.psum_scatter(partial_terms, 'ffn', scatter_dimension=0, tiled=True)[0]  8.84 us
    ppermute x4, starting transfers between devices, swap_cores(): return lax.ppermute(value, 'expert', [(0, 1), (1, 0)])  8.74 us
    pallas_call x1, Pallas kernels, weight_grads(): pl.pallas_call(weight_grad_kernel, grid=(experts,), in_specs=[pl.BlockSpe...  5.1 us
  transfers between devices with their start and end apart: 9, of which 4 were waited for; matrix products, arithmetic and copies ran while one was open for 2% of the time, Pallas kernels for 12%

profile of v5, /device:TPU:6, one launch (start us, length us, event | category | flops | bytes accessed | tf_op | source)
XLA Modules:
  0.0 135.8 jit_solution(9188165749286036687)
XLA Ops:
  7.2 0.0 all-gather.2.cloned.1.call-start
  7.2 2.1 %prepare.1 = (bf16[8,392,128]{2,1,0:T(8,128)(2,1)}, bf16[2,288,256]{2,1,0:T(8,128)(2,1)}) custom-call(s32[1]{0:T(128)} %bitcast.core_ref, bf16[128,768]{1,0:T(8,128)(2,1)} %rows_ref.1, s32[2,128]{1,0:T(2,128)} %bitcast.14, f32[2,128]{1,0:T(2,128)} %bitcast.15, bf16[2,288,256]{2,1,0:T(8,128)(2,1)} %gate_ref.3, bf16[2,288,256]{2,1,0:T(8,128)(2,1)} %up_ref.3), custom_call_target="tpu_custom_call" | custom-call | tf_op jit(solution)/shard_map/prepare/pallas_call | solution.py:46
  9.4 0.0 all-gather.2.cloned.1.call-update
  9.4 0.0 reduce-scatter.2.cloned.1.call-start
  9.4 30.6 %all_to_all.15.own_ref = bf16[8,392,128]{2,1,0:T(8,128)(2,1)S(1)} all-to-all(bf16[8,392,128]{2,1,0:T(8,128)(2,1)} %get-tuple-element.24), channel_id=1, replica_groups=mesh['x'=4,'y'=8,'expert'=2,'ffn'=8] {'y'}, dimensions={0} | all-to-all | bytes 1605632 | tf_op jit(solution)/shard_map/all_to_all | solution.py:279
  40.0 1.9 %collective-permute-start.1 = (bf16[8,392,128]{2,1,0:T(8,128)(2,1)S(1)}, bf16[8,392,128]{2,1,0:T(8,128)(2,1)S(1)}, u32[]{:S(2)}, u32[]{:S(2)}) collective-permute-start(bf16[8,392,128]{2,1,0:T(8,128)(2,1)S(1)} %all_to_all.15.own_ref), channel_id=1, source_target_pairs={{0,8},{8,0},{1,9},{9,1},{2,10},{10,2},{3,11},{11,3},{4,12},{12,4},... | collective-permute-start | bytes 2408456 | tf_op jit(solution)/shard_map/ppermute | solution.py:287
  41.9 2.4 %collective-permute-start = (bf16[8,392,128]{2,1,0:T(8,128)(2,1)S(1)}, bf16[8,392,128]{2,1,0:T(8,128)(2,1)S(1)}, u32[]{:S(2)}, u32[]{:S(2)}) collective-permute-start(bf16[8,392,128]{2,1,0:T(8,128)(2,1)S(1)} %all_to_all.15.own_ref), channel_id=1, source_target_pairs={{0,128},{8,392},{128,256},{136,8},{256,384},{264,136},{384,0},{392... | collective-permute-start | bytes 2408456 | tf_op jit(solution)/shard_map/ppermute | solution.py:296
  44.3 1.4 %copy.17 = bf16[2,256,768]{1,2,0:T(8,128)(2,1)S(1)} copy(bf16[2,256,768]{2,1,0:T(8,128)(2,1)} %param.11) | data formatting | bytes 1572864 | tf_op args[5]
  45.8 0.1 stack.20.place_ref
  45.9 3.4 %collective-permute-start.3 = (bf16[8,392,128]{2,1,0:T(8,128)(2,1)S(1)}, bf16[8,392,128]{2,1,0:T(8,128)(2,1)S(1)}, u32[]{:S(2)}, u32[]{:S(2)}) collective-permute-start(bf16[8,392,128]{2,1,0:T(8,128)(2,1)S(1)} %collective-permute-done.1.other_ref), channel_id=1, source_target_pairs={{0,128},{8,392},{128,256},{136,8},{256,384},{264,136},{384,0},{392... | collective-permute-start | bytes 2408456 | tf_op jit(solution)/shard_map/ppermute | solution.py:296
  49.3 2.7 %dispatch_project.4 = (bf16[2,2304,768]{2,1,0:T(8,128)(2,1)}, bf16[8,2,288,256]{3,2,1,0:T(8,128)(2,1)}) custom-call(s32[5]{0:T(128)S(1)} %stack.20.place_ref, bf16[8,392,128]{2,1,0:T(8,128)(2,1)S(1)} %all_to_all.15.own_ref, bf16[8,392,128]{2,1,0:T(8,128)(2,1)S(1)} %collective-permute-done.1.other_ref, bf16[2,768,256]{2,1,0:T(8,128)(2,1)S(1)} %bitcast.9), custom_call_target="tpu_custom_call" | custom-call | tf_op jit(solution)/shard_map/dispatch_project/pallas_call | solution.py:207
  52.0 4.0 %collective-permute-done.own_ref = bf16[8,392,128]{2,1,0:T(8,128)(2,1)S(1)} collective-permute-done((bf16[8,392,128]{2,1,0:T(8,128)(2,1)S(1)}, bf16[8,392,128]{2,1,0:T(8,128)(2,1)S(1)}, u32[]{:S(2)}, u32[]{:S(2)}) %collective-permute-start) | collective-permute-done | bytes 802848 | tf_op jit(solution)/shard_map/ppermute | solution.py:296
  56.0 3.6 %collective-permute-start.2 = (bf16[8,392,128]{2,1,0:T(8,128)(2,1)S(1)}, bf16[8,392,128]{2,1,0:T(8,128)(2,1)S(1)}, u32[]{:S(2)}, u32[]{:S(2)}) collective-permute-start(bf16[8,392,128]{2,1,0:T(8,128)(2,1)S(1)} %collective-permute-done.own_ref), channel_id=1, source_target_pairs={{0,128},{8,392},{128,256},{136,8},{256,384},{264,136},{384,0},{392... | collective-permute-start | bytes 2408456 | tf_op jit(solution)/shard_map/ppermute | solution.py:296
  59.6 1.9 %collective-permute-start.6 = (bf16[8,392,128]{2,1,0:T(8,128)(2,1)S(1)}, bf16[8,392,128]{2,1,0:T(8,128)(2,1)S(1)}, u32[]{:S(2)}, u32[]{:S(2)}) collective-permute-start(bf16[8,392,128]{2,1,0:T(8,128)(2,1)S(1)} %collective-permute-done.own_ref), channel_id=1, source_target_pairs={{0,8},{8,0},{1,9},{9,1},{2,10},{10,2},{3,11},{11,3},{4,12},{12,4},... | collective-permute-start | bytes 2408456 | tf_op jit(solution)/shard_map/ppermute | solution.py:287
  61.5 3.1 %collective-permute-done.3.other_ref = bf16[8,392,128]{2,1,0:T(8,128)(2,1)S(1)} collective-permute-done((bf16[8,392,128]{2,1,0:T(8,128)(2,1)S(1)}, bf16[8,392,128]{2,1,0:T(8,128)(2,1)S(1)}, u32[]{:S(2)}, u32[]{:S(2)}) %collective-permute-start.3) | collective-permute-done | bytes 802848 | tf_op jit(solution)/shard_map/ppermute | solution.py:296
  64.6 2.5 %collective-permute-start.5 = (bf16[8,392,128]{2,1,0:T(8,128)(2,1)S(1)}, bf16[8,392,128]{2,1,0:T(8,128)(2,1)S(1)}, u32[]{:S(2)}, u32[]{:S(2)}) collective-permute-start(bf16[8,392,128]{2,1,0:T(8,128)(2,1)S(1)} %collective-permute-done.3.other_ref), channel_id=1, source_target_pairs={{0,8},{8,0},{1,9},{9,1},{2,10},{10,2},{3,11},{11,3},{4,12},{12,4},... | collective-permute-start | bytes 2408456 | tf_op jit(solution)/shard_map/ppermute | solution.py:287
  67.0 2.7 %dispatch_project.5 = (bf16[2,2304,768]{2,1,0:T(8,128)(2,1)}, bf16[8,2,288,256]{3,2,1,0:T(8,128)(2,1)}) custom-call(s32[5]{0:T(128)S(1)} %stack.20.place_ref, bf16[8,392,128]{2,1,0:T(8,128)(2,1)S(1)} %collective-permute-done.own_ref, bf16[8,392,128]{2,1,0:T(8,128)(2,1)S(1)} %collective-permute-done.3.other_ref, ...), custom_call_target="tpu_custom_call", output_to_operand_aliasing={{0}: (4, {}), {1}: (5, {})} | custom-call | tf_op jit(solution)/shard_map/dispatch_project/pallas_call | solution.py:207
  69.7 3.5 %collective-permute-done.2.own_ref = bf16[8,392,128]{2,1,0:T(8,128)(2,1)S(1)} collective-permute-done((bf16[8,392,128]{2,1,0:T(8,128)(2,1)S(1)}, bf16[8,392,128]{2,1,0:T(8,128)(2,1)S(1)}, u32[]{:S(2)}, u32[]{:S(2)}) %collective-permute-start.2) | collective-permute-done | bytes 802848 | tf_op jit(solution)/shard_map/ppermute | solution.py:296
  73.2 2.5 %collective-permute-start.4 = (bf16[8,392,128]{2,1,0:T(8,128)(2,1)S(1)}, bf16[8,392,128]{2,1,0:T(8,128)(2,1)S(1)}, u32[]{:S(2)}, u32[]{:S(2)}) collective-permute-start(bf16[8,392,128]{2,1,0:T(8,128)(2,1)S(1)} %collective-permute-done.2.own_ref), channel_id=1, source_target_pairs={{0,8},{8,0},{1,9},{9,1},{2,10},{10,2},{3,11},{11,3},{4,12},{12,4},... | collective-permute-start | bytes 2408456 | tf_op jit(solution)/shard_map/ppermute | solution.py:287
  75.7 2.7 %dispatch_project.6 = (bf16[2,2304,768]{2,1,0:T(8,128)(2,1)}, bf16[8,2,288,256]{3,2,1,0:T(8,128)(2,1)}) custom-call(s32[5]{0:T(128)S(1)} %stack.20.place_ref, bf16[8,392,128]{2,1,0:T(8,128)(2,1)S(1)} %collective-permute-done.5.own_ref, bf16[8,392,128]{2,1,0:T(8,128)(2,1)S(1)} %collective-permute-done.6.other_ref, ...), custom_call_target="tpu_custom_call", output_to_operand_aliasing={{0}: (4, {}), {1}: (5, {})} | custom-call | tf_op jit(solution)/shard_map/dispatch_project/pallas_call | solution.py:207
  78.4 2.7 %dispatch_project.7 = (bf16[2,2304,768]{2,1,0:T(8,128)(2,1)}, bf16[8,2,288,256]{3,2,1,0:T(8,128)(2,1)}) custom-call(s32[5]{0:T(128)S(1)} %stack.20.place_ref, bf16[8,392,128]{2,1,0:T(8,128)(2,1)S(1)} %collective-permute-done.2.own_ref, bf16[8,392,128]{2,1,0:T(8,128)(2,1)S(1)} %collective-permute-done.4.other_ref, ...), custom_call_target="tpu_custom_call", output_to_operand_aliasing={{0}: (4, {}), {1}: (5, {})} | custom-call | tf_op jit(solution)/shard_map/dispatch_project/pallas_call | solution.py:207
  81.1 0.0 reduce-scatter.2.cloned.1.call-update
  81.1 0.0 all-gather.2.cloned.1.call-done.hidden_ref
  81.1 5.1 %weight_grads.1 = (f32[2,256,768]{2,1,0:T(8,128)S(1)}, f32[32,1,128]{2,1,0:T(1,128)S(1)}) custom-call(bf16[2,2304,256]{2,1,0:T(8,128)(2,1)} %all-gather.2.cloned.1.call-done.hidden_ref, bf16[2,2304,768]{2,1,0:T(8,128)(2,1)} %get-tuple-element.37.placed_ref), custom_call_target="tpu_custom_call" | custom-call | tf_op jit(solution)/shard_map/weight_grads/pallas_call | solution.py:252
  86.3 12.6 %all_to_all.16 = f32[32,1,128]{2,1,0:T(1,128)S(1)} all-to-all(f32[32,1,128]{2,1,0:T(1,128)S(1)} %get-tuple-element.39), channel_id=1, replica_groups=mesh['x'=4,'y'=8,'expert'=2,'ffn'=8] {'x','y'}, dimensions={0} | all-to-all | bytes 32768 | tf_op jit(solution)/shard_map/all_to_all | solution.py:279
  98.8 0.1 reduce_sum.18
  98.9 17.8 %all_to_all.17 = f32[16,1,128]{2,1,0:T(1,128)S(1)} all-to-all(f32[16,1,128]{2,1,0:T(1,128)S(1)} %broadcast_in_dim.2), channel_id=1, replica_groups=mesh['x'=4,'y'=8,'expert'=2,'ffn'=8] {'expert','ffn'}, dimensions={0} | all-to-all | bytes 16384 | tf_op jit(solution)/shard_map/all_to_all | solution.py:279
  116.7 0.6 slice_reduce_fusion
  118.1 0.1 multiply_convert_fusion.after_ref
  118.2 0.0 copy-start
  118.2 8.8 %reduce-scatter.2.cloned.1.call-done = bf16[1,2,288,256]{3,2,1,0:T(8,128)(2,1)} async-done(((bf16[8,2,288,256]{3,2,1,0:T(8,128)(2,1)}), bf16[1,2,288,256]{3,2,1,0:T(8,128)(2,1)}) %reduce-scatter.2.cloned.1.call-update) | async-done | bytes 294928 | tf_op jit(solution)/shard_map/reduce_scatter | solution.py:337
  127.0 1.9 %gate_up_grads.1 = (bf16[2,288,256]{2,1,0:T(8,128)(2,1)}, bf16[2,288,256]{2,1,0:T(8,128)(2,1)}) custom-call(bf16[2,288,256]{2,1,0:T(8,128)(2,1)} %bitcast.13, bf16[2,288,256]{2,1,0:T(8,128)(2,1)S(1)} %copy-done.1, bf16[2,288,256]{2,1,0:T(8,128)(2,1)S(1)} %copy-done.2, bf16[2,256,768]{2,1,0:T(8,128)(2,1)S(1)} %multiply_convert_fusion.after_ref), custom_call_target="tpu_custom_call" | custom-call | tf_op jit(solution)/shard_map/gate_up_grads/pallas_call | solution.py:97
  (10 shorter events, 0.0 us)
Async XLA Ops:
  7.2 74.0 %all-gather.2.cloned.1.call-start = ((), (), s32[]{:S(2)}) async-start(), calls=%async_computation.4 | async-start | bytes 2654208 | tf_op jit(solution)/shard_map/all_gather | solution.py:314
  9.4 117.6 %reduce-scatter.2.cloned.1.call-start = ((), (), s32[]{:S(2)}) async-start(), calls=%async_computation.5 | async-start | bytes 2654208 | tf_op jit(solution)/shard_map/reduce_scatter | solution.py:337
  40.0 5.9 %collective-permute-start.1 = (bf16[8,392,128]{2,1,0:T(8,128)(2,1)S(1)}, bf16[8,392,128]{2,1,0:T(8,128)(2,1)S(1)}, u32[]{:S(2)}, u32[]{:S(2)}) collective-permute-start(bf16[8,392,128]{2,1,0:T(8,128)(2,1)S(1)} %all_to_all.15.own_ref), channel_id=1, source_target_pairs={{0,8},{8,0},{1,9},{9,1},{2,10},{10,2},{3,11},{11,3},{4,12},{12,4},... | collective-permute-start | bytes 2408456 | tf_op jit(solution)/shard_map/ppermute | solution.py:287
  41.9 14.1 %collective-permute-start = (bf16[8,392,128]{2,1,0:T(8,128)(2,1)S(1)}, bf16[8,392,128]{2,1,0:T(8,128)(2,1)S(1)}, u32[]{:S(2)}, u32[]{:S(2)}) collective-permute-start(bf16[8,392,128]{2,1,0:T(8,128)(2,1)S(1)} %all_to_all.15.own_ref), channel_id=1, source_target_pairs={{0,128},{8,392},{128,256},{136,8},{256,384},{264,136},{384,0},{392... | collective-permute-start | bytes 2408456 | tf_op jit(solution)/shard_map/ppermute | solution.py:296
  45.9 18.7 %collective-permute-start.3 = (bf16[8,392,128]{2,1,0:T(8,128)(2,1)S(1)}, bf16[8,392,128]{2,1,0:T(8,128)(2,1)S(1)}, u32[]{:S(2)}, u32[]{:S(2)}) collective-permute-start(bf16[8,392,128]{2,1,0:T(8,128)(2,1)S(1)} %collective-permute-done.1.other_ref), channel_id=1, source_target_pairs={{0,128},{8,392},{128,256},{136,8},{256,384},{264,136},{384,0},{392... | collective-permute-start | bytes 2408456 | tf_op jit(solution)/shard_map/ppermute | solution.py:296
  56.0 17.2 %collective-permute-start.2 = (bf16[8,392,128]{2,1,0:T(8,128)(2,1)S(1)}, bf16[8,392,128]{2,1,0:T(8,128)(2,1)S(1)}, u32[]{:S(2)}, u32[]{:S(2)}) collective-permute-start(bf16[8,392,128]{2,1,0:T(8,128)(2,1)S(1)} %collective-permute-done.own_ref), channel_id=1, source_target_pairs={{0,128},{8,392},{128,256},{136,8},{256,384},{264,136},{384,0},{392... | collective-permute-start | bytes 2408456 | tf_op jit(solution)/shard_map/ppermute | solution.py:296
  59.6 16.1 %collective-permute-start.6 = (bf16[8,392,128]{2,1,0:T(8,128)(2,1)S(1)}, bf16[8,392,128]{2,1,0:T(8,128)(2,1)S(1)}, u32[]{:S(2)}, u32[]{:S(2)}) collective-permute-start(bf16[8,392,128]{2,1,0:T(8,128)(2,1)S(1)} %collective-permute-done.own_ref), channel_id=1, source_target_pairs={{0,8},{8,0},{1,9},{9,1},{2,10},{10,2},{3,11},{11,3},{4,12},{12,4},... | collective-permute-start | bytes 2408456 | tf_op jit(solution)/shard_map/ppermute | solution.py:287
  64.6 11.1 %collective-permute-start.5 = (bf16[8,392,128]{2,1,0:T(8,128)(2,1)S(1)}, bf16[8,392,128]{2,1,0:T(8,128)(2,1)S(1)}, u32[]{:S(2)}, u32[]{:S(2)}) collective-permute-start(bf16[8,392,128]{2,1,0:T(8,128)(2,1)S(1)} %collective-permute-done.3.other_ref), channel_id=1, source_target_pairs={{0,8},{8,0},{1,9},{9,1},{2,10},{10,2},{3,11},{11,3},{4,12},{12,4},... | collective-permute-start | bytes 2408456 | tf_op jit(solution)/shard_map/ppermute | solution.py:287
  73.2 5.2 %collective-permute-start.4 = (bf16[8,392,128]{2,1,0:T(8,128)(2,1)S(1)}, bf16[8,392,128]{2,1,0:T(8,128)(2,1)S(1)}, u32[]{:S(2)}, u32[]{:S(2)}) collective-permute-start(bf16[8,392,128]{2,1,0:T(8,128)(2,1)S(1)} %collective-permute-done.2.own_ref), channel_id=1, source_target_pairs={{0,8},{8,0},{1,9},{9,1},{2,10},{10,2},{3,11},{11,3},{4,12},{12,4},... | collective-permute-start | bytes 2408456 | tf_op jit(solution)/shard_map/ppermute | solution.py:287
  86.2 40.8 %copy-start.1 = (bf16[2,288,256]{2,1,0:T(8,128)(2,1)S(1)}, bf16[2,288,256]{2,1,0:T(8,128)(2,1)}, u32[]{:S(2)}) copy-start(bf16[2,288,256]{2,1,0:T(8,128)(2,1)} %gate_ref.3) | copy-start | bytes 884740
  86.3 40.8 %copy-start.2 = (bf16[2,288,256]{2,1,0:T(8,128)(2,1)S(1)}, bf16[2,288,256]{2,1,0:T(8,128)(2,1)}, u32[]{:S(2)}) copy-start(bf16[2,288,256]{2,1,0:T(8,128)(2,1)} %up_ref.3) | copy-start | bytes 884740
  118.2 10.8 %copy-start = (bf16[2,256,768]{2,1,0:T(8,128)(2,1)}, bf16[2,256,768]{2,1,0:T(8,128)(2,1)S(1)}, u32[]{:S(2)}) copy-start(bf16[2,256,768]{2,1,0:T(8,128)(2,1)S(1)} %multiply_convert_fusion.after_ref) | copy-start | bytes 2359300
Sparse Core Ops, SparseCore 0:
  10.7 49.6 all-gather.1
  81.2 45.7 reduce-scatter.1

commit v6 on v4

--- a/solution.py
+++ b/solution.py
@@ -284,7 +284,6 @@
     payload, hidden = prepare(core, grad_rows, expert_ids, gate_probs, gate_pre, up_pre, lines)
     near = exchange(payload, "y")
     hidden_all = lax.all_gather(hidden, "ffn", axis=1, tiled=True)
-    weight = jnp.swapaxes(down_weight, 1, 2)
     offsets = [0, planes - 1 + 2 * core, 1 + planes - 2 * core, 2]
     places = jnp.stack([(plane + offset) % planes for offset in offsets] + [core]).astype(jnp.int32)
 
@@ -296,8 +295,9 @@
     side_own = along_x(near)
     near_other = swap_cores(near)
     side_other = along_x(near_other)
+    side_own, down_weight = lax.optimization_barrier((side_own, down_weight))
+    weight = jnp.swapaxes(down_weight, 1, 2)
     buffers = project(0, near, near_other, ())
-    side_own, buffers = lax.optimization_barrier((side_own, buffers))
     far_own = along_x(side_own)
     beyond_other = swap_cores(side_own)
     beyond_own = swap_cores(side_other)

time: 136 us -> 137 us (level)
  Pallas kernels: 20 us -> 21.9 us
    pallas_call x4, Pallas kernels: 10.7 us -> 12.6 us  [dispatch_and_project(): pl.pallas_call(functools.partial(dispatch_kernel, turn), in_specs=[pl.Blo...]
    unnamed x7 -> x6, local copies, waits for them, and re-layouts: 1.44 us -> 0.02 us
    optimization_barrier x0 -> x1, local copies, waits for them, and re-layouts: none -> 1.4 us  [on_device(): side_own, down_weight = lax.optimization_barrier((side_own, down_weight))]
  transfers between devices with their start and end apart: 9 -> 9, of which waited for: 4 -> 3; matrix products, arithmetic and copies ran while one was open for 2% -> 2% of each run, Pallas kernels for 12% -> 13%
where the time goes in v6:
time: 137 us
  blocking collectives  61 us (45%)
  Pallas kernels  21.9 us (16%)
  waiting for transfers between devices  18.3 us (13%)
  starting transfers between devices  18.1 us (13%)
  between operations  15 us (11%)
  local copies, waits for them, and re-layouts  1.52 us (1%)
    all_to_all x3, blocking collectives, exchange(): return lax.all_to_all(value, axis, 0, 0, tiled=True)  61 us
    pallas_call x4, Pallas kernels, dispatch_and_project(): pl.pallas_call(functools.partial(dispatch_kernel, turn), in_specs=[pl.Blo...  12.6 us
    ppermute x3, waiting for transfers between devices, along_x(): return lax.ppermute(value, ('x', 'expert'), pairs)  9.39 us
    ppermute x3, starting transfers between devices, along_x(): return lax.ppermute(value, ('x', 'expert'), pairs)  9.37 us
    reduce_scatter x1, waiting for transfers between devices, on_device(): lax.psum_scatter(partial_terms, 'ffn', scatter_dimension=0, tiled=True)[0]  8.82 us
    ppermute x4, starting transfers between devices, swap_cores(): return lax.ppermute(value, 'expert', [(0, 1), (1, 0)])  8.69 us
    pallas_call x1, Pallas kernels, weight_grads(): pl.pallas_call(weight_grad_kernel, grid=(experts,), in_specs=[pl.BlockSpe...  5.09 us
  transfers between devices with their start and end apart: 9, of which 3 were waited for; matrix products, arithmetic and copies ran while one was open for 2% of the time, Pallas kernels for 13%

profile of v6, /device:TPU:6, one launch (start us, length us, event | category | flops | bytes accessed | tf_op | source)
XLA Modules:
  0.0 136.5 jit_solution(8783564306401721408)
XLA Ops:
  7.2 0.0 all-gather.2.cloned.1.call-start
  7.2 2.3 %prepare.1 = (bf16[8,392,128]{2,1,0:T(8,128)(2,1)}, bf16[2,288,256]{2,1,0:T(8,128)(2,1)}) custom-call(s32[1]{0:T(128)} %bitcast.core_ref, bf16[128,768]{1,0:T(8,128)(2,1)} %rows_ref.1, s32[2,128]{1,0:T(2,128)} %bitcast.14, f32[2,128]{1,0:T(2,128)} %bitcast.15, bf16[2,288,256]{2,1,0:T(8,128)(2,1)} %gate_ref.3, bf16[2,288,256]{2,1,0:T(8,128)(2,1)} %up_ref.3), custom_call_target="tpu_custom_call" | custom-call | tf_op jit(solution)/shard_map/prepare/pallas_call | solution.py:53
  9.5 0.0 all-gather.2.cloned.1.call-update
  9.5 0.0 reduce-scatter.2.cloned.1.call-start
  9.6 30.6 %all_to_all.15.own_ref = bf16[8,392,128]{2,1,0:T(8,128)(2,1)S(1)} all-to-all(bf16[8,392,128]{2,1,0:T(8,128)(2,1)} %get-tuple-element.23), channel_id=1, replica_groups=mesh['x'=4,'y'=8,'expert'=2,'ffn'=8] {'y'}, dimensions={0} | all-to-all | bytes 1605632 | tf_op jit(solution)/shard_map/all_to_all | solution.py:251
  40.1 1.9 %collective-permute-start.2 = (bf16[8,392,128]{2,1,0:T(8,128)(2,1)S(1)}, bf16[8,392,128]{2,1,0:T(8,128)(2,1)}, u32[]{:S(2)}, u32[]{:S(2)}) collective-permute-start(bf16[8,392,128]{2,1,0:T(8,128)(2,1)S(1)} %all_to_all.15.own_ref), channel_id=1, source_target_pairs={{0,8},{8,0},{1,9},{9,1},{2,10},{10,2},{3,11},{11,3},{4,12},{12,4},... | collective-permute-start | bytes 2408456 | tf_op jit(solution)/shard_map/ppermute | solution.py:259
  42.0 2.4 %collective-permute-start = (bf16[8,392,128]{2,1,0:T(8,128)(2,1)S(1)}, bf16[8,392,128]{2,1,0:T(8,128)(2,1)S(1)}, u32[]{:S(2)}, u32[]{:S(2)}) collective-permute-start(bf16[8,392,128]{2,1,0:T(8,128)(2,1)S(1)} %all_to_all.15.own_ref), channel_id=1, source_target_pairs={{0,128},{8,392},{128,256},{136,8},{256,384},{264,136},{384,0},{392... | collective-permute-start | bytes 2408456 | tf_op jit(solution)/shard_map/ppermute | solution.py:268
  44.4 0.0 collective-permute-done.2.other_ref
  44.5 3.4 %collective-permute-start.3 = (bf16[8,392,128]{2,1,0:T(8,128)(2,1)}, bf16[8,392,128]{2,1,0:T(8,128)(2,1)}, u32[]{:S(2)}, u32[]{:S(2)}) collective-permute-start(bf16[8,392,128]{2,1,0:T(8,128)(2,1)} %collective-permute-done.2.other_ref), channel_id=1, source_target_pairs={{0,128},{8,392},{128,256},{136,8},{256,384},{264,136},{384,0},{392... | collective-permute-start | bytes 2408456 | tf_op jit(solution)/shard_map/ppermute | solution.py:268
  47.9 8.2 %collective-permute-done.own_ref = bf16[8,392,128]{2,1,0:T(8,128)(2,1)S(1)} collective-permute-done((bf16[8,392,128]{2,1,0:T(8,128)(2,1)S(1)}, bf16[8,392,128]{2,1,0:T(8,128)(2,1)S(1)}, u32[]{:S(2)}, u32[]{:S(2)}) %collective-permute-start) | collective-permute-done | bytes 802848 | tf_op jit(solution)/shard_map/ppermute | solution.py:268
  56.1 3.6 %collective-permute-start.1 = (bf16[8,392,128]{2,1,0:T(8,128)(2,1)S(1)}, bf16[8,392,128]{2,1,0:T(8,128)(2,1)S(1)}, u32[]{:S(2)}, u32[]{:S(2)}) collective-permute-start(bf16[8,392,128]{2,1,0:T(8,128)(2,1)S(1)} %collective-permute-done.own_ref), channel_id=1, source_target_pairs={{0,128},{8,392},{128,256},{136,8},{256,384},{264,136},{384,0},{392... | collective-permute-start | bytes 2408456 | tf_op jit(solution)/shard_map/ppermute | solution.py:268
  59.7 0.1 stack.20.place_ref
  59.8 1.9 %collective-permute-start.6 = (bf16[8,392,128]{2,1,0:T(8,128)(2,1)S(1)}, bf16[8,392,128]{2,1,0:T(8,128)(2,1)}, u32[]{:S(2)}, u32[]{:S(2)}) collective-permute-start(bf16[8,392,128]{2,1,0:T(8,128)(2,1)S(1)} %collective-permute-done.own_ref), channel_id=1, source_target_pairs={{0,8},{8,0},{1,9},{9,1},{2,10},{10,2},{3,11},{11,3},{4,12},{12,4},... | collective-permute-start | bytes 2408456 | tf_op jit(solution)/shard_map/ppermute | solution.py:259
  61.7 1.4 %copy.17 = bf16[2,256,768]{1,2,0:T(8,128)(2,1)S(1)} copy(bf16[2,256,768]{2,1,0:T(8,128)(2,1)} %param.11) | data formatting | bytes 1572864 | tf_op jit(solution)/shard_map/optimization_barrier | solution.py:298
  63.2 3.3 %dispatch_project.4 = (bf16[2,2304,768]{2,1,0:T(8,128)(2,1)}, bf16[8,2,288,256]{3,2,1,0:T(8,128)(2,1)}) custom-call(s32[5]{0:T(128)S(1)} %stack.20.place_ref, bf16[8,392,128]{2,1,0:T(8,128)(2,1)S(1)} %all_to_all.15.own_ref, bf16[8,392,128]{2,1,0:T(8,128)(2,1)} %collective-permute-done.2.other_ref, bf16[2,768,256]{2,1,0:T(8,128)(2,1)S(1)} %bitcast.9), custom_call_target="tpu_custom_call" | custom-call | tf_op jit(solution)/shard_map/dispatch_project/pallas_call | solution.py:179
  66.5 2.4 %collective-permute-start.5 = (bf16[8,392,128]{2,1,0:T(8,128)(2,1)}, bf16[8,392,128]{2,1,0:T(8,128)(2,1)S(1)}, u32[]{:S(2)}, u32[]{:S(2)}) collective-permute-start(bf16[8,392,128]{2,1,0:T(8,128)(2,1)} %collective-permute-done.3.other_ref), channel_id=1, source_target_pairs={{0,8},{8,0},{1,9},{9,1},{2,10},{10,2},{3,11},{11,3},{4,12},{12,4},... | collective-permute-start | bytes 2408456 | tf_op jit(solution)/shard_map/ppermute | solution.py:259
  68.9 3.3 %dispatch_project.5 = (bf16[2,2304,768]{2,1,0:T(8,128)(2,1)}, bf16[8,2,288,256]{3,2,1,0:T(8,128)(2,1)}) custom-call(s32[5]{0:T(128)S(1)} %stack.20.place_ref, bf16[8,392,128]{2,1,0:T(8,128)(2,1)S(1)} %collective-permute-done.own_ref, bf16[8,392,128]{2,1,0:T(8,128)(2,1)} %collective-permute-done.3.other_ref, ...), custom_call_target="tpu_custom_call", output_to_operand_aliasing={{0}: (4, {}), {1}: (5, {})} | custom-call | tf_op jit(solution)/shard_map/dispatch_project/pallas_call | solution.py:179
  72.2 1.1 collective-permute-done.1.own_ref
  73.3 2.5 %collective-permute-start.4 = (bf16[8,392,128]{2,1,0:T(8,128)(2,1)S(1)}, bf16[8,392,128]{2,1,0:T(8,128)(2,1)S(1)}, u32[]{:S(2)}, u32[]{:S(2)}) collective-permute-start(bf16[8,392,128]{2,1,0:T(8,128)(2,1)S(1)} %collective-permute-done.1.own_ref), channel_id=1, source_target_pairs={{0,8},{8,0},{1,9},{9,1},{2,10},{10,2},{3,11},{11,3},{4,12},{12,4},... | collective-permute-start | bytes 2408456 | tf_op jit(solution)/shard_map/ppermute | solution.py:259
  75.8 3.3 %dispatch_project.6 = (bf16[2,2304,768]{2,1,0:T(8,128)(2,1)}, bf16[8,2,288,256]{3,2,1,0:T(8,128)(2,1)}) custom-call(s32[5]{0:T(128)S(1)} %stack.20.place_ref, bf16[8,392,128]{2,1,0:T(8,128)(2,1)S(1)} %collective-permute-done.5.own_ref, bf16[8,392,128]{2,1,0:T(8,128)(2,1)} %collective-permute-done.6.other_ref, ...), custom_call_target="tpu_custom_call", output_to_operand_aliasing={{0}: (4, {}), {1}: (5, {})} | custom-call | tf_op jit(solution)/shard_map/dispatch_project/pallas_call | solution.py:179
  79.1 2.7 %dispatch_project.7 = (bf16[2,2304,768]{2,1,0:T(8,128)(2,1)}, bf16[8,2,288,256]{3,2,1,0:T(8,128)(2,1)}) custom-call(s32[5]{0:T(128)S(1)} %stack.20.place_ref, bf16[8,392,128]{2,1,0:T(8,128)(2,1)S(1)} %collective-permute-done.1.own_ref, bf16[8,392,128]{2,1,0:T(8,128)(2,1)S(1)} %collective-permute-done.4.other_ref, ...), custom_call_target="tpu_custom_call", output_to_operand_aliasing={{0}: (4, {}), {1}: (5, {})} | custom-call | tf_op jit(solution)/shard_map/dispatch_project/pallas_call | solution.py:179
  81.8 0.0 reduce-scatter.2.cloned.1.call-update
  81.8 0.0 all-gather.2.cloned.1.call-done.hidden_ref
  81.9 5.1 %weight_grads.1 = (f32[2,256,768]{2,1,0:T(8,128)S(1)}, f32[32,1,128]{2,1,0:T(1,128)S(1)}) custom-call(bf16[2,2304,256]{2,1,0:T(8,128)(2,1)} %all-gather.2.cloned.1.call-done.hidden_ref, bf16[2,2304,768]{2,1,0:T(8,128)(2,1)} %get-tuple-element.35.placed_ref), custom_call_target="tpu_custom_call" | custom-call | tf_op jit(solution)/shard_map/weight_grads/pallas_call | solution.py:224
  87.0 12.5 %all_to_all.16 = f32[32,1,128]{2,1,0:T(1,128)S(1)} all-to-all(f32[32,1,128]{2,1,0:T(1,128)S(1)} %get-tuple-element.37), channel_id=1, replica_groups=mesh['x'=4,'y'=8,'expert'=2,'ffn'=8] {'x','y'}, dimensions={0} | all-to-all | bytes 32768 | tf_op jit(solution)/shard_map/all_to_all | solution.py:251
  99.6 0.1 reduce_sum.18
  99.6 17.8 %all_to_all.17 = f32[16,1,128]{2,1,0:T(1,128)S(1)} all-to-all(f32[16,1,128]{2,1,0:T(1,128)S(1)} %broadcast_in_dim.2), channel_id=1, replica_groups=mesh['x'=4,'y'=8,'expert'=2,'ffn'=8] {'expert','ffn'}, dimensions={0} | all-to-all | bytes 16384 | tf_op jit(solution)/shard_map/all_to_all | solution.py:251
  117.4 0.6 slice_reduce_fusion
  118.8 0.1 multiply_convert_fusion.after_ref
  118.9 0.0 copy-start
  118.9 8.8 %reduce-scatter.2.cloned.1.call-done = bf16[1,2,288,256]{3,2,1,0:T(8,128)(2,1)} async-done(((bf16[8,2,288,256]{3,2,1,0:T(8,128)(2,1)}), bf16[1,2,288,256]{3,2,1,0:T(8,128)(2,1)}) %reduce-scatter.2.cloned.1.call-update) | async-done | bytes 294928 | tf_op jit(solution)/shard_map/reduce_scatter | solution.py:309
  127.7 1.9 %gate_up_grads.1 = (bf16[2,288,256]{2,1,0:T(8,128)(2,1)}, bf16[2,288,256]{2,1,0:T(8,128)(2,1)}) custom-call(bf16[2,288,256]{2,1,0:T(8,128)(2,1)} %bitcast.13, bf16[2,288,256]{2,1,0:T(8,128)(2,1)S(1)} %copy-done.1, bf16[2,288,256]{2,1,0:T(8,128)(2,1)S(1)} %copy-done.2, bf16[2,256,768]{2,1,0:T(8,128)(2,1)S(1)} %multiply_convert_fusion.after_ref), custom_call_target="tpu_custom_call" | custom-call | tf_op jit(solution)/shard_map/gate_up_grads/pallas_call | solution.py:75
  (10 shorter events, 0.0 us)
Async XLA Ops:
  7.2 74.7 %all-gather.2.cloned.1.call-start = ((), (), s32[]{:S(2)}) async-start(), calls=%async_computation.4 | async-start | bytes 2654208 | tf_op jit(solution)/shard_map/all_gather | solution.py:286
  9.5 118.2 %reduce-scatter.2.cloned.1.call-start = ((), (), s32[]{:S(2)}) async-start(), calls=%async_computation.5 | async-start | bytes 2654208 | tf_op jit(solution)/shard_map/reduce_scatter | solution.py:309
  40.1 4.3 %collective-permute-start.2 = (bf16[8,392,128]{2,1,0:T(8,128)(2,1)S(1)}, bf16[8,392,128]{2,1,0:T(8,128)(2,1)}, u32[]{:S(2)}, u32[]{:S(2)}) collective-permute-start(bf16[8,392,128]{2,1,0:T(8,128)(2,1)S(1)} %all_to_all.15.own_ref), channel_id=1, source_target_pairs={{0,8},{8,0},{1,9},{9,1},{2,10},{10,2},{3,11},{11,3},{4,12},{12,4},... | collective-permute-start | bytes 2408456 | tf_op jit(solution)/shard_map/ppermute | solution.py:259
  42.0 14.1 %collective-permute-start = (bf16[8,392,128]{2,1,0:T(8,128)(2,1)S(1)}, bf16[8,392,128]{2,1,0:T(8,128)(2,1)S(1)}, u32[]{:S(2)}, u32[]{:S(2)}) collective-permute-start(bf16[8,392,128]{2,1,0:T(8,128)(2,1)S(1)} %all_to_all.15.own_ref), channel_id=1, source_target_pairs={{0,128},{8,392},{128,256},{136,8},{256,384},{264,136},{384,0},{392... | collective-permute-start | bytes 2408456 | tf_op jit(solution)/shard_map/ppermute | solution.py:268
  44.5 22.0 %collective-permute-start.3 = (bf16[8,392,128]{2,1,0:T(8,128)(2,1)}, bf16[8,392,128]{2,1,0:T(8,128)(2,1)}, u32[]{:S(2)}, u32[]{:S(2)}) collective-permute-start(bf16[8,392,128]{2,1,0:T(8,128)(2,1)} %collective-permute-done.2.other_ref), channel_id=1, source_target_pairs={{0,128},{8,392},{128,256},{136,8},{256,384},{264,136},{384,0},{392... | collective-permute-start | bytes 2408456 | tf_op jit(solution)/shard_map/ppermute | solution.py:268
  56.1 17.2 %collective-permute-start.1 = (bf16[8,392,128]{2,1,0:T(8,128)(2,1)S(1)}, bf16[8,392,128]{2,1,0:T(8,128)(2,1)S(1)}, u32[]{:S(2)}, u32[]{:S(2)}) collective-permute-start(bf16[8,392,128]{2,1,0:T(8,128)(2,1)S(1)} %collective-permute-done.own_ref), channel_id=1, source_target_pairs={{0,128},{8,392},{128,256},{136,8},{256,384},{264,136},{384,0},{392... | collective-permute-start | bytes 2408456 | tf_op jit(solution)/shard_map/ppermute | solution.py:268
  59.8 15.9 %collective-permute-start.6 = (bf16[8,392,128]{2,1,0:T(8,128)(2,1)S(1)}, bf16[8,392,128]{2,1,0:T(8,128)(2,1)}, u32[]{:S(2)}, u32[]{:S(2)}) collective-permute-start(bf16[8,392,128]{2,1,0:T(8,128)(2,1)S(1)} %collective-permute-done.own_ref), channel_id=1, source_target_pairs={{0,8},{8,0},{1,9},{9,1},{2,10},{10,2},{3,11},{11,3},{4,12},{12,4},... | collective-permute-start | bytes 2408456 | tf_op jit(solution)/shard_map/ppermute | solution.py:259
  66.5 9.3 %collective-permute-start.5 = (bf16[8,392,128]{2,1,0:T(8,128)(2,1)}, bf16[8,392,128]{2,1,0:T(8,128)(2,1)S(1)}, u32[]{:S(2)}, u32[]{:S(2)}) collective-permute-start(bf16[8,392,128]{2,1,0:T(8,128)(2,1)} %collective-permute-done.3.other_ref), channel_id=1, source_target_pairs={{0,8},{8,0},{1,9},{9,1},{2,10},{10,2},{3,11},{11,3},{4,12},{12,4},... | collective-permute-start | bytes 2408456 | tf_op jit(solution)/shard_map/ppermute | solution.py:259
  73.3 5.8 %collective-permute-start.4 = (bf16[8,392,128]{2,1,0:T(8,128)(2,1)S(1)}, bf16[8,392,128]{2,1,0:T(8,128)(2,1)S(1)}, u32[]{:S(2)}, u32[]{:S(2)}) collective-permute-start(bf16[8,392,128]{2,1,0:T(8,128)(2,1)S(1)} %collective-permute-done.1.own_ref), channel_id=1, source_target_pairs={{0,8},{8,0},{1,9},{9,1},{2,10},{10,2},{3,11},{11,3},{4,12},{12,4},... | collective-permute-start | bytes 2408456 | tf_op jit(solution)/shard_map/ppermute | solution.py:259
  87.0 40.8 %copy-start.1 = (bf16[2,288,256]{2,1,0:T(8,128)(2,1)S(1)}, bf16[2,288,256]{2,1,0:T(8,128)(2,1)}, u32[]{:S(2)}) copy-start(bf16[2,288,256]{2,1,0:T(8,128)(2,1)} %gate_ref.3) | copy-start | bytes 884740
  87.0 40.8 %copy-start.2 = (bf16[2,288,256]{2,1,0:T(8,128)(2,1)S(1)}, bf16[2,288,256]{2,1,0:T(8,128)(2,1)}, u32[]{:S(2)}) copy-start(bf16[2,288,256]{2,1,0:T(8,128)(2,1)} %up_ref.3) | copy-start | bytes 884740
  118.9 10.8 %copy-start = (bf16[2,256,768]{2,1,0:T(8,128)(2,1)}, bf16[2,256,768]{2,1,0:T(8,128)(2,1)S(1)}, u32[]{:S(2)}) copy-start(bf16[2,256,768]{2,1,0:T(8,128)(2,1)S(1)} %multiply_convert_fusion.after_ref) | copy-start | bytes 2359300
Sparse Core Ops, SparseCore 0:
  10.7 49.6 all-gather.1
  82.0 45.7 reduce-scatter.1
